TPU v7x, 32 devices: a whole 2x2x4 slice. The times are simulated.
32 devices in a mesh: dp: 4 (over y, x), space: 8 (over z, core).
Axes of the slice: x: 2, y: 2, z: 4, core: 2. Of those that a mesh axis runs over, the one named last changes fastest.
Arguments:
- volumes: bfloat16 [4, 4, 64, 32, 512], P('dp', None, 'space'), may hold values from -6 to 6
- first_kernel: bfloat16 [3, 3, 3, 4, 32], replicated, may hold values from -0.625 to 0.625
- second_kernel: float32 [3, 3, 3, 32, 64], replicated, may hold values from -0.21875 to 0.21875
- cotangent: bfloat16 [4, 64, 16, 8, 128], P('dp', None, 'space'), may hold values from -0.5 to 0.5
- first_moment: float32 [55296], P(('dp', 'space')), may hold values from -0.75 to 0.75
- second_moment: float32 [55296], P(('dp', 'space')), may hold values from 0.001 to 0.01
Outputs:
- activations: bfloat16 [4, 64, 16, 8, 128], P('dp', None, 'space')
- first_gradient: float32 [3, 3, 3, 4, 32], replicated
- new_kernel: float32 [3, 3, 3, 32, 64], replicated
- new_first_moment: float32 [55296], P(('dp', 'space'))
- new_second_moment: float32 [55296], P(('dp', 'space'))
All inputs are finite; a program needn't handle non-finite values.
Results may differ from a plain program's by a relative error of at most 0.0055.
The roundings to bfloat16 on the way count: a program that leaves them out, or rounds other values in their place, can miss the bound.
Values may be sent and summed in bfloat16 or wider, within the bound.
No kernel may reach another device: no remote copies, remote signals or barrier semaphores. Data moves between devices by JAX's collectives and lax.ppermute only.
A program may use at most 256 MiB of HBM per device.

v0:
```python
import jax
import jax.numpy as jnp
from jax import lax
from jax.sharding import PartitionSpec as P

SLOPE = 0.3
BETA_FIRST = 0.9
BETA_SECOND = 0.999
LEARN_RATE = 0.001
EPSILON = 1e-08
NUMBERS = ("NCDHW", "DHWIO", "NCDHW")


def from_behind(value, axis, steps):
    count = lax.axis_size(axis)
    first, last = (max(0, -steps), min(count, count - steps))
    return lax.ppermute(value, axis, [(source, source + steps) for source in range(first, last)])


def strided(inputs, kernel):
    return lax.conv_general_dilated(
        inputs,
        kernel,
        (2, 2, 2),
        [(0, 0), (1, 1), (1, 1)],
        dimension_numbers=NUMBERS,
        preferred_element_type=jnp.float32,
    )


def strided_exact(inputs, kernel, depth_pad):
    return lax.conv_general_dilated(
        inputs,
        kernel,
        (2, 2, 2),
        [depth_pad, (1, 1), (1, 1)],
        dimension_numbers=NUMBERS,
        preferred_element_type=jnp.float32,
    )


def leaky(values):
    return jnp.where(values > 0, values, SLOPE * values)


def leaky_slope(values):
    return jnp.where(values > 0, jnp.float32(1.0), jnp.float32(SLOPE))


def shards(volumes, first_kernel, second_kernel, cotangent, first_moment, second_moment):
    lower_plane = from_behind(volumes[:, :, -1:], "space", 1)
    padded_in = jnp.concatenate([lower_plane, volumes], axis=2)
    preact_one = strided(padded_in, first_kernel)
    hidden = leaky(preact_one).astype(jnp.bfloat16)
    lower_hidden = from_behind(hidden[:, :, -1:], "space", 1)
    padded_hidden = jnp.concatenate([lower_hidden, hidden], axis=2)
    kernel_half = second_kernel.astype(jnp.bfloat16)
    preact_two = strided(padded_hidden, kernel_half)
    activations = leaky(preact_two).astype(jnp.bfloat16)
    delta_two = (cotangent.astype(jnp.float32) * leaky_slope(preact_two)).astype(jnp.bfloat16)
    second_wide = kernel_half.astype(jnp.float32)
    hidden_wide = padded_hidden.astype(jnp.float32)
    delta_wide = delta_two.astype(jnp.float32)

    def second_map(activ, kernel):
        return strided_exact(activ, kernel, (0, 0))

    _, pull_second = jax.vjp(second_map, hidden_wide, second_wide)
    grad_padded, second_gradient = pull_second(delta_wide)
    returned = from_behind(grad_padded[:, :, :1], "space", -1)
    grad_hidden = jnp.concatenate(
        [grad_padded[:, :, 1:-1], grad_padded[:, :, -1:] + returned], axis=2
    )
    delta_one = (grad_hidden * leaky_slope(preact_one)).astype(jnp.bfloat16)
    inputs_wide = padded_in.astype(jnp.float32)

    def first_map(kernel):
        return strided_exact(inputs_wide, kernel, (0, 0))

    _, pull_first = jax.vjp(first_map, first_kernel.astype(jnp.float32))
    (first_local,) = pull_first(delta_one.astype(jnp.float32))
    flat_grad = second_gradient.reshape(-1)
    share = first_moment.shape[0]
    offset = lax.axis_index(("dp", "space")) * share
    total_second, first_gradient = lax.psum((flat_grad, first_local), ("dp", "space"))
    grad_share = lax.dynamic_slice_in_dim(total_second, offset, share, 0)
    new_first = BETA_FIRST * first_moment + (1.0 - BETA_FIRST) * grad_share
    new_second = BETA_SECOND * second_moment + (1.0 - BETA_SECOND) * grad_share * grad_share
    kernel_share = lax.dynamic_slice_in_dim(second_kernel.reshape(-1), offset, share, 0)
    updated_share = kernel_share - LEARN_RATE * new_first / (jnp.sqrt(new_second) + EPSILON)
    new_kernel = lax.all_gather(updated_share, ("dp", "space"), axis=0, tiled=True).reshape(
        second_kernel.shape
    )
    return (activations, first_gradient, new_kernel, new_first, new_second)


def solution(mesh):
    in_specs = (
        P("dp", None, "space", None, None),
        P(),
        P(),
        P("dp", None, "space", None, None),
        P(("dp", "space")),
        P(("dp", "space")),
    )
    out_specs = (
        P("dp", None, "space", None, None),
        P(),
        P(),
        P(("dp", "space")),
        P(("dp", "space")),
    )
    return jax.shard_map(shards, mesh=mesh, in_specs=in_specs, out_specs=out_specs, check_vma=False)
```

profile of v0, /device:TPU:0, one launch (start us, length us, event | category | flops | bytes accessed | tf_op | source)
XLA Modules:
  0.0 863.4 jit_solution(15912801684704176963)
XLA Ops:
  8.2 2.4 collective-permute-start
  12.4 2.1 copy.76
  18.8 3.9 reshape.24
  22.7 19.7 %copy.66 = bf16[4,9,32,1,8,66]{4,0,5,2,1,3:T(4,128)(2,1)} copy(bf16[4,9,32,1,8,66]{5,4,2,1,0,3:T(8,128)(2,1)S(1)} %reshape.24) | data formatting | bytes 2433024 | tf_op jit(solution)/shard_map/conv_general_dilated | solution.py:21
  43.9 63.5 %compare_select_fusion = (f32[4,16,8,33,32]{4,2,3,1,0:T(8,128)}, bf16[4,16,8,33,32]{4,2,3,1,0:T(8,128)(2,1)S(1)}) fusion(pred[8,33]{0,1:T(8,128)(4,1)S(1)} %copy-done.12, bf16[3,3,3,4,32]{4,3,2,1,0:T(4,128)(2,1)S(1)} %copy-done, bf16[4,9,32,1,7,2]{4,0,5,2,1,3:T(4,128)(2,1)S(1)} %slice.35, bf16[4,9,32,1,8,66]{4,0,5,2,1,3:T(4,128)(2,1)} %copy.66), kind=kOutput, calls=%fused_computation.8 | convolution fusion | flops 121356288 | bytes 4499976 | tf_op jit(solution)/shard_map/conv_general_dilated | solution.py:21
  107.6 3.9 copy.90
  113.8 4.6 collective-permute-start.1
  118.4 24.8 %reshape.72 = bf16[4,16,1,264,32]{4,2,3,1,0:T(2,128)(2,1)} reshape(bf16[4,16,8,33,32]{4,3,2,1,0:T(8,128)(2,1)} %copy.90) | data formatting | bytes 2162688 | tf_op jit(solution)/shard_map/convert_element_type | solution.py:54
  143.3 11.1 %slice_bitcast_fusion = bf16[1,32,4,16,256]{1,0,4,3,2:T(2,128)(2,1)} fusion(bf16[4,16,1,264,32]{4,2,3,1,0:T(2,128)(2,1)} %reshape.72), kind=kLoop, calls=%fused_computation.12 | loop fusion | bytes 2097152 | tf_op jit(solution)/shard_map/convert_element_type | solution.py:54
  154.4 80.1 %copy.86 = bf16[1,4,9,32,512]{1,0,4,3,2:T(2,128)(2,1)} copy(bf16[1,4,9,32,512]{4,3,2,1,0:T(8,128)(2,1)S(1)} %copy-done.4) | data formatting | bytes 2359296 | tf_op jit(solution)/shard_map/concatenate | solution.py:52
  234.5 10.7 %copy.85 = f32[4,16,8,33,32]{3,2,4,1,0:T(8,128)} copy(f32[4,16,8,33,32]{4,2,3,1,0:T(8,128)} %get-tuple-element.25) | data formatting | bytes 4325376 | tf_op jit(solution)/shard_map/jit(_where)/select_n | solution.py:47
  245.2 7.4 reshape.52
  253.8 32.8 %pad_maximum_fusion = bf16[1,32,5,16,256]{1,0,4,3,2:T(2,128)(2,1)} fusion(bf16[1,32,4,16,256]{1,0,4,3,2:T(2,128)(2,1)} %slice_bitcast_fusion, bf16[1,32,1,16,256]{1,0,4,3,2:T(2,128)(2,1)S(1)} %copy.71), kind=kLoop, calls=%fused_computation.9 | loop fusion | flops 655360 | bytes 2621440 | tf_op jit(solution)/shard_map/concatenate | solution.py:56
  286.6 13.3 %copy.72 = bf16[1,32,5,16,256]{4,3,2,1,0:T(8,128)(2,1)S(1)} copy(bf16[1,32,5,16,256]{1,0,4,3,2:T(2,128)(2,1)} %pad_maximum_fusion) | data formatting | bytes 2621440 | tf_op jit(solution)/shard_map/concatenate | solution.py:56
  300.7 5.6 reshape.31
  306.3 10.2 %copy.74 = bf16[32,5,16,1,8,34]{0,4,5,2,1,3:T(8,128)(2,1)} copy(bf16[32,5,16,1,8,34]{5,4,2,1,0,3:T(8,128)(2,1)} %reshape.31) | data formatting | bytes 2785280 | tf_op jit(solution)/shard_map/conv_general_dilated | solution.py:21
  317.8 7.2 compare_select_fusion.1
  325.4 25.6 %fusion.22 = f32[3,3,3,32,64]{4,3,2,1,0:T(8,128)S(1)} fusion(bf16[1,32,5,16,256]{1,0,4,3,2:T(2,128)(2,1)S(1)} %bitcast.86, bf16[1,64,2,8,128]{1,3,4,2,0:T(8,128)(2,1)S(1)} %fusion.21), kind=kOutput, calls=%fused_computation.31 | convolution fusion | flops 216489984 | bytes 1794048 | tf_op jit(solution)/shard_map/transpose(jvp())/conv_general_dilated | solution.py:32
  351.2 5.3 broadcast_select_fusion
  358.2 3.4 slice.43
  362.5 8.3 copy.80
  370.8 5.9 reshape.50
  376.7 3.3 copy.83
  384.3 2.8 slice_bitcast_fusion.2
  388.2 97.7 %all-reduce.4.cloned.1.call-done = f32[55296]{0:T(1024)} async-done(((f32[55296]{0:T(1024)}), f32[55296]{0:T(1024)}) %all-reduce.4.cloned.1.call-update) | async-done | bytes 221200 | tf_op jit(solution)/shard_map/psum | solution.py:85
  489.3 2.4 copy.81
  491.7 3.0 reshape.48
  494.6 121.4 %all-reduce.6.cloned.1.call-done = f32[55296]{0:T(1024)} async-done(((f32[55296]{0:T(1024)}), f32[55296]{0:T(1024)}) %all-reduce.6.cloned.1.call-update) | async-done | bytes 221200
  619.1 2.8 fusion.14
  621.9 18.4 %copy.87 = bf16[1,32,4,16,256]{1,0,4,3,2:T(2,128)(2,1)} copy(bf16[1,32,4,16,256]{4,1,3,2,0:T(8,128)(2,1)} %fusion.14) | data formatting | bytes 2097152 | tf_op jit(solution)/shard_map/convert_element_type | solution.py:74
  640.3 173.7 %fusion.46 = f32[3,3,3,4,32]{4,3,2,1,0:T(4,128)S(1)} fusion(bf16[1,4,9,32,512]{1,0,4,3,2:T(2,128)(2,1)} %copy.86, bf16[1,32,4,16,256]{1,0,4,3,2:T(2,128)(2,1)} %copy.87), kind=kOutput, calls=%fused_computation.62 | convolution fusion | flops 110742528 | bytes 2242048 | tf_op jit(solution)/shard_map/transpose(jvp())/conv_general_dilated | solution.py:32
  814.1 42.3 %psum.14 = f32[3,3,3,4,32]{4,3,2,1,0:T(4,128)} all-reduce(f32[3,3,3,4,32]{4,3,2,1,0:T(4,128)S(1)} %fusion.46), channel_id=1, replica_groups=mesh['dp'=4,'space'=8] {'dp','space'}, use_global_device_ids=true, to_apply=%region_0.1 | all-reduce | flops 3456 | bytes 27648 | tf_op jit(solution)/shard_map/psum | solution.py:85
  (73 shorter events, 29.1 us)
Async XLA Ops:
  7.2 36.8 %copy-start = (bf16[3,3,3,4,32]{4,3,2,1,0:T(4,128)(2,1)S(1)}, bf16[3,3,3,4,32]{4,3,2,1,0:T(4,128)(2,1)}, u32[]{:S(2)}) copy-start(bf16[3,3,3,4,32]{4,3,2,1,0:T(4,128)(2,1)} %param.7) | copy-start | bytes 20740
  7.2 478.7 %all-reduce.4.cloned.1.call-start = ((), (), s32[]{:S(2)}) async-start(), calls=%async_computation | async-start | bytes 442368 | tf_op jit(solution)/shard_map/psum | solution.py:85
  8.2 6.3 collective-permute-start
  15.8 1.1 copy-start.3
  22.7 21.2 %copy-start.12 = (pred[8,33]{0,1:T(8,128)(4,1)S(1)}, pred[8,33]{0,1:T(8,128)(4,1)}, u32[]{:S(2)}) copy-start(pred[8,33]{0,1:T(8,128)(4,1)} %constant.50) | copy-start | bytes 796
  113.8 138.8 %collective-permute-start.1 = (bf16[1,32,1,16,256]{4,3,2,1,0:T(8,128)(2,1)S(1)}, bf16[1,32,1,16,256]{4,3,2,1,0:T(8,128)(2,1)S(1)}, u32[]{:S(2)}, u32[]{:S(2)}) collective-permute-start(bf16[1,32,1,16,256]{4,3,2,1,0:T(8,128)(2,1)S(1)} %copy.68), channel_id=1, source_target_pairs={{0,1},{1,2},{2,3},{3,4},{4,5},{5,6},{6,7},{8,9},{9,10},{10,11},{11... | collective-permute-start | bytes 786440 | tf_op jit(solution)/shard_map/ppermute | solution.py:17
  143.3 11.1 %copy-start.4 = (bf16[1,4,9,32,512]{4,3,2,1,0:T(8,128)(2,1)S(1)}, bf16[1,4,9,32,512]{4,3,2,1,0:T(8,128)(2,1)}, u32[]{:S(2)}) copy-start(bf16[1,4,9,32,512]{4,3,2,1,0:T(8,128)(2,1)} %copy-done.3) | copy-start | bytes 3538948
  306.3 11.4 %copy-start.7 = (f32[3,3,3,32,64]{4,3,2,1,0:T(8,128)S(1)}, f32[3,3,3,32,64]{4,3,2,1,0:T(8,128)}, u32[]{:S(2)}) copy-start(f32[3,3,3,32,64]{4,3,2,1,0:T(8,128)} %param.8) | copy-start | bytes 663556
  306.3 11.4 %copy-start.13 = (pred[8,17]{0,1:T(8,128)(4,1)S(1)}, pred[8,17]{0,1:T(8,128)(4,1)}, u32[]{:S(2)}) copy-start(pred[8,17]{0,1:T(8,128)(4,1)} %constant.49) | copy-start | bytes 412
  316.5 8.8 %slice-start = ((s8[10485760]{0:T(1024)(128)(4,1)}), s8[4194304]{0:T(1024)(128)(4,1)S(1)}, s32[]{:S(2)}) async-start(s8[10485760]{0:T(1024)(128)(4,1)} %bitcast.85), calls=%async_computation.2 | async-start | bytes 8388608
  317.7 7.5 copy-start.5
  317.7 7.6 slice-start.1
  317.7 7.6 slice-start.2
  325.3 25.8 %copy-start.8 = (f32[3,3,3,32,64]{4,3,2,1,0:T(8,128)S(1)}, f32[3,3,3,32,64]{4,3,2,1,0:T(8,128)}, u32[]{:S(2)}) copy-start(f32[3,3,3,32,64]{4,3,2,1,0:T(8,128)} %param.8) | copy-start | bytes 663556
  325.4 25.8 %copy-start.11 = (pred[8,34]{0,1:T(8,128)(4,1)S(1)}, pred[8,34]{0,1:T(8,128)(4,1)}, u32[]{:S(2)}) copy-start(pred[8,34]{0,1:T(8,128)(4,1)} %constant.51) | copy-start | bytes 820
  362.4 253.6 %all-reduce.6.cloned.1.call-start = ((), (), s32[]{:S(2)}) async-start(), calls=%async_computation.1 | async-start | bytes 442368
  376.7 109.2 %copy-start.9 = (f32[1728]{0:T(1024)S(1)}, f32[1728]{0:T(1024)}, u32[]{:S(2)}) copy-start(f32[1728]{0:T(1024)} %param.10) | copy-start | bytes 20740
  376.7 109.2 %copy-start.10 = (f32[1728]{0:T(1024)S(1)}, f32[1728]{0:T(1024)}, u32[]{:S(2)}) copy-start(f32[1728]{0:T(1024)} %param.11) | copy-start | bytes 20740
  383.0 234.9 %collective-permute-start.2 = (f32[1,32,1,16,256]{4,1,3,2,0:T(8,128)}, f32[1,32,1,16,256]{4,1,3,2,0:T(8,128)}, u32[]{:S(2)}, u32[]{:S(2)}) collective-permute-start(f32[1,32,1,16,256]{4,1,3,2,0:T(8,128)} %slice_bitcast_fusion.4), channel_id=1, source_target_pairs={{1,0},{2,1},{3,2},{4,3},{5,4},{6,5},{7,6},{9,8},{10,9},{11,10},{12... | collective-permute-start | bytes 1572872 | tf_op jit(solution)/shard_map/ppermute | solution.py:17
  487.4 0.7 copy-start.6
  491.7 127.5 %copy-start.2 = (f32[4,16,1,264,32]{3,4,1,0,2:T(8,128)S(1)}, f32[4,16,1,264,32]{3,4,1,0,2:T(8,128)}, u32[]{:S(2)}) copy-start(f32[4,16,1,264,32]{3,4,1,0,2:T(8,128)} %reshape.52) | copy-start | bytes 6488068
  640.3 216.0 %copy-start.1 = (bf16[3,3,3,4,32]{4,3,2,1,0:T(4,128)(2,1)S(1)}, bf16[3,3,3,4,32]{4,3,2,1,0:T(4,128)(2,1)}, u32[]{:S(2)}) copy-start(bf16[3,3,3,4,32]{4,3,2,1,0:T(4,128)(2,1)} %param.7) | copy-start | bytes 20740
Sparse Core Ops, SparseCore 0:
  362.6 123.2 all-reduce.3
  492.0 123.9 all-reduce.5
where the time goes:
time: 877 us; the launch traced here: 863 us
  matrix products  275 us (31%)
  local copies, waits for them, and re-layouts  265 us (30%)
  waiting for transfers between devices  219 us (25%)
  blocking collectives  42.3 us (5%)
  other arithmetic  38.4 us (4%)
  between operations  14.7 us (2%)
    conv_general_dilated x3, matrix products, strided_exact(): lax.conv_general_dilated(inputs, kernel, (2, 2, 2), [depth_pad, (1, 1), (...  205 us
    unnamed x3, waiting for transfers between devices  121 us
    psum x1, waiting for transfers between devices, shards(): lax.psum((flat_grad, first_local), ('dp', 'space'))  97.7 us
    concatenate x3, local copies, waits for them, and re-layouts, shards(): padded_in = jnp.concatenate([lower_plane, volumes], axis=2)  83.2 us
    conv_general_dilated x2, matrix products, strided(): lax.conv_general_dilated(inputs, kernel, (2, 2, 2), [(0, 0), (1, 1), (1,...  70.8 us
    psum x1, blocking collectives, shards(): lax.psum((flat_grad, first_local), ('dp', 'space'))  42.3 us
    conv_general_dilated x6, local copies, waits for them, and re-layouts, strided(): lax.conv_general_dilated(inputs, kernel, (2, 2, 2), [(0, 0), (1, 1), (1,...  42.1 us
    convert_element_type x6, local copies, waits for them, and re-layouts, shards(): hidden = leaky(preact_one).astype(jnp.bfloat16)  42.1 us
  transfers between devices with their start and end apart: 5, of which 2 were waited for; matrix products, arithmetic and copies ran while one was open for 20% of the time, Pallas kernels for 0%

commit v1 on v0

v1 whole, which is shorter than its diff:
```python
import jax
import jax.numpy as jnp
import numpy as np
from jax import lax
from jax.experimental import pallas as pl
from jax.experimental.pallas import tpu as pltpu
from jax.sharding import PartitionSpec as P

SLOPE = 0.3
BETA_FIRST = 0.9
BETA_SECOND = 0.999
LEARN_RATE = 0.001
EPSILON = 1e-08
BF = jnp.bfloat16
F32 = jnp.float32
AXES = ("dp", "space")
LANES = 128


def along(value, axis, steps):
    count = lax.axis_size(axis)
    first, last = (max(0, -steps), min(count, count - steps))
    return lax.ppermute(value, axis, [(source, source + steps) for source in range(first, last)])


def leaky(values):
    return jnp.where(values > 0, values, SLOPE * values)


def nn(a, b):
    return lax.dot_general(a, b, (((1,), (0,)), ((), ())), preferred_element_type=F32)


def nt(a, b):
    return lax.dot_general(a, b, (((1,), (1,)), ((), ())), preferred_element_type=F32)


def tn(a, b):
    return lax.dot_general(a, b, (((0,), (0,)), ((), ())), preferred_element_type=F32)


def spread_taps():
    table = np.zeros((3, 3, 4, 2, 2, 256), np.float32)
    for dy in range(3):
        for dx in range(3):
            for c in range(4):
                for row in range(2):
                    for p in range(2):
                        table[dy, dx, c, row, p, (2 * row + dy) * 32 + (2 * p + dx) * 4 + c] = 1
    return table.reshape(36, 1024)


def forward_kernel(v_ref, vh_ref, w1_ref, e_ref, w2_ref, cot_ref,
                   act_ref, d_ref, h_ref, d2_ref, edge_ref,
                   sel, stage, t1, rows_c, rows_a):
    lane = lax.broadcasted_iota(jnp.int32, (512, LANES), 1)
    row = lax.broadcasted_iota(jnp.int32, (512, LANES), 0)
    base = row - 4 * lane
    for r in range(5):
        sel[:, r * LANES:(r + 1) * LANES] = jnp.where(base == r - 1, 1.0, 0.0).astype(BF)
    for dz in range(3):
        taps = tn(w1_ref[dz], e_ref[...]).astype(BF)
        for b in range(4):
            t1[dz, b * 32:(b + 1) * 32, :] = taps[:, b * 256:b * 256 + 160]
    stage[...] = jnp.zeros_like(stage)
    lane32 = lax.broadcasted_iota(jnp.int32, (32, LANES), 1)

    def plane(source, z, out):
        x = source[:, z].reshape(128, 512)
        parts = nn(x, sel[...])
        for r in range(5):
            for c in range(4):
                stage[pl.ds(32 + r * 4 + c, 32, stride=32), :] = parts[c * 32:(c + 1) * 32, r * LANES:(r + 1) * LANES]
        d_ref[out] = stage[...].astype(BF)

    @pl.loop(0, 3)
    def _(z):
        plane(vh_ref, z, z)

    @pl.loop(0, 8)
    def _(z):
        plane(v_ref, z, z + 3)

    @pl.loop(0, 5)
    def _(z):
        h_ref[z, 0:96] = jnp.zeros((96, LANES), BF)
        for m in range(8):
            acc = nn(t1[0], d_ref[2 * z, m * 128:m * 128 + 160])
            acc += nn(t1[1], d_ref[2 * z + 1, m * 128:m * 128 + 160])
            acc += nn(t1[2], d_ref[2 * z + 2, m * 128:m * 128 + 160])
            hid = leaky(acc)
            for i in range(2):
                at = (2 * m + i + 1) * 96
                odd = hid[i * 64 + 32:i * 64 + 64]
                h_ref[z, at:at + 32] = jnp.where(lane32 == 0, 0.0, pltpu.roll(odd, 1, 1)).astype(BF)
                h_ref[z, at + 32:at + 96] = hid[i * 64:i * 64 + 64].astype(BF)

    lane64 = lax.broadcasted_iota(jnp.int32, (64, LANES), 1)
    for z in range(2):
        rows_c[...] = cot_ref[:, z].astype(F32).reshape(512, LANES)
        d2_ref[z, 1024:1152] = jnp.zeros((128, LANES), BF)
        for y in range(8):
            acc = nn(w2_ref[0], h_ref[2 * z, y * 192:y * 192 + 288])
            acc += nn(w2_ref[1], h_ref[2 * z + 1, y * 192:y * 192 + 288])
            acc += nn(w2_ref[2], h_ref[2 * z + 2, y * 192:y * 192 + 288])
            rows_a[pl.ds(y, 64, stride=8), :] = leaky(acc)
            cot = rows_c[pl.ds(y, 64, stride=8), :]
            delta = cot * jnp.where(acc > 0, 1.0, SLOPE)
            low = delta.astype(BF)
            d2_ref[z, y * 128:y * 128 + 64] = low
            if z == 0:
                edge_ref[y * 64:y * 64 + 64] = low
            left = jnp.where(lane64 == LANES - 1, 0.0, pltpu.roll(delta, LANES - 1, 1))
            d2_ref[z, y * 128 + 64:y * 128 + 128] = left.astype(BF)
        act_ref[:, z] = rows_a[...].astype(BF).reshape(64, 8, LANES)


def backward_kernel(d_ref, h_ref, d2_ref, above_ref, l_ref, g2_ref, g1_ref, d2h, d1):
    lane64 = lax.broadcasted_iota(jnp.int32, (64, LANES), 1)
    d2h[1024:1152] = jnp.zeros((128, LANES), BF)
    for y in range(8):
        low = above_ref[y * 64:y * 64 + 64]
        left = jnp.where(lane64 == LANES - 1, 0.0, pltpu.roll(low.astype(F32), LANES - 1, 1))
        d2h[y * 128:y * 128 + 64] = low
        d2h[y * 128 + 64:y * 128 + 128] = left.astype(BF)

    for dz in range(3):
        acc = jnp.zeros((288, 64), F32)
        for y in range(8):
            a = jnp.concatenate([h_ref[dz, y * 192:y * 192 + 288], h_ref[dz + 2, y * 192:y * 192 + 288]], axis=1)
            b = jnp.concatenate([d2_ref[0, y * 128:y * 128 + 64], d2_ref[1, y * 128:y * 128 + 64]], axis=1)
            acc += nt(a, b)
        g2_ref[dz] = acc

    def slope(z, m):
        parts = [jnp.where(h_ref[z + 1, (2 * m + i + 1) * 96 + 32:(2 * m + i + 1) * 96 + 96].astype(F32) > 0, 1.0, SLOPE) for i in range(2)]
        return jnp.concatenate(parts, axis=0)

    for m in range(8):
        r0 = nn(l_ref[128:384], d2_ref[0, m * 128:m * 128 + 256])
        r1 = nn(l_ref[...], d2_ref[1, m * 128:m * 128 + 256])
        r2 = nn(l_ref[0:128], d2h[m * 128:m * 128 + 256])
        grads = (r0[0:128], r0[128:256] + r1[0:128], r1[128:256], r1[256:384] + r2)
        for z in range(4):
            d1[z, m * 128:m * 128 + 128] = (grads[z] * slope(z, m)).astype(BF)

    for dz in range(3):
        acc = jnp.zeros((160, LANES), F32)
        for m in range(8):
            for zz in range(2):
                z = 2 * zz
                a = jnp.concatenate([d_ref[2 * z + 2 + dz, m * 128:m * 128 + 160], d_ref[2 * z + 4 + dz, m * 128:m * 128 + 160]], axis=1)
                b = jnp.concatenate([d1[z, m * 128:m * 128 + 128], d1[z + 1, m * 128:m * 128 + 128]], axis=1)
                acc += nt(a, b)
        for dy in range(3):
            total = jnp.zeros((16, LANES), F32)
            for i in range(2):
                for p in range(2):
                    at = (2 * i + dy) * 32 + 8 * p
                    block = acc[at:at + 16]
                    shift = (2 * i + p) * 32
                    total += block if shift == 0 else pltpu.roll(block, LANES - shift, 1)
            g1_ref[dz * 3 + dy] = total[0:12, 0:32]


VMEM = pl.BlockSpec(memory_space=pltpu.VMEM)


def call(kernel, outs, scratch, args):
    return pl.pallas_call(
        kernel,
        out_shape=[jax.ShapeDtypeStruct(s, t) for s, t in outs],
        in_specs=[VMEM] * len(args),
        out_specs=[VMEM] * len(outs),
        scratch_shapes=scratch,
        compiler_params=pltpu.CompilerParams(vmem_limit_bytes=56 * 1024 * 1024),
    )(*args)


def scatter_sum(values):
    return lax.all_to_all(values, AXES, 0, 0, tiled=True).sum(0)


def gather(values, count):
    wide = jnp.broadcast_to(values[None], (count,) + values.shape)
    return lax.all_to_all(wide, AXES, 0, 0, tiled=True)


def shards(volumes, first_kernel, second_kernel, cotangent, first_moment, second_moment):
    count = lax.axis_size(AXES)
    below = along(volumes[0, :, -3:], "space", 1)
    kernel_half = second_kernel.astype(BF)
    w2 = kernel_half.reshape(3, 288, 64).transpose(0, 2, 1)
    zero = jnp.zeros((3, 32, 64), BF)
    tap = lambda dy, dx: kernel_half[:, dy, dx]
    lines = (
        (tap(1, 1), zero, zero, zero),
        (tap(1, 2), tap(1, 0), zero, zero),
        (tap(2, 1), zero, tap(0, 1), zero),
        (tap(2, 2), tap(2, 0), tap(0, 2), tap(0, 0)),
    )
    back = jnp.concatenate([jnp.concatenate(line, axis=2) for line in lines], axis=1).reshape(384, 256)
    act, d, h, d2, edge = call(
        forward_kernel,
        [((64, 2, 8, LANES), BF), ((11, 1056, LANES), BF), ((5, 1632, LANES), BF), ((2, 1152, LANES), BF), ((512, LANES), BF)],
        [pltpu.VMEM((512, 640), BF), pltpu.VMEM((1056, LANES), F32), pltpu.VMEM((3, 128, 160), BF),
         pltpu.VMEM((512, LANES), F32), pltpu.VMEM((512, LANES), F32)],
        (volumes[0], below, first_kernel.reshape(3, 36, 32), jnp.asarray(spread_taps(), BF), w2, cotangent[0]),
    )
    above = along(edge, "space", -1)
    g2, g1 = call(
        backward_kernel,
        [((3, 288, 64), F32), ((9, 12, 32), F32)],
        [pltpu.VMEM((1152, LANES), BF), pltpu.VMEM((4, 1024, LANES), BF)],
        (d, h, d2, above, back),
    )
    share = first_moment.shape[0]
    one = g1.reshape(-1)
    pad = -one.shape[0] % count
    one = jnp.pad(one, (0, pad)).reshape(count, -1)
    both = scatter_sum(jnp.concatenate([g2.reshape(count, share), one], axis=1))
    grad_share = both[:share]
    offset = lax.axis_index(AXES) * share
    new_first = BETA_FIRST * first_moment + (1.0 - BETA_FIRST) * grad_share
    new_second = BETA_SECOND * second_moment + (1.0 - BETA_SECOND) * grad_share * grad_share
    kernel_share = lax.dynamic_slice_in_dim(second_kernel.reshape(-1), offset, share, 0)
    updated = kernel_share - LEARN_RATE * new_first / (jnp.sqrt(new_second) + EPSILON)
    full = gather(jnp.concatenate([updated, both[share:]]), count)
    new_kernel = full[:, :share].reshape(second_kernel.shape)
    first_gradient = full[:, share:].reshape(-1)[:first_kernel.size].reshape(first_kernel.shape)
    return (act[None], first_gradient, new_kernel, new_first, new_second)


def solution(mesh):
    field = P("dp", None, "space", None, None)
    flat = P(AXES)
    return jax.shard_map(
        shards, mesh=mesh, in_specs=(field, P(), P(), field, flat, flat),
        out_specs=(field, P(), P(), flat, flat), check_vma=False)
```

time: 877 us -> 71.9 us (0.08); the launches traced: 863 us -> 71.3 us
  matrix products: 275 us -> 0 us
  local copies, waits for them, and re-layouts: 265 us -> 9.85 us
  waiting for transfers between devices: 219 us -> 14.5 us
  other arithmetic: 38.4 us -> 2.79 us
  blocking collectives: 42.3 us -> 12.4 us
  Pallas kernels: 0 us -> 18.6 us
  between operations: 14.7 us -> 0.76 us
    conv_general_dilated x5 -> x0, matrix products: 275 us -> none  [the longest x3 205 us: strided_exact(): lax.conv_general_dilated(inputs, kernel, (2, 2, 2), [depth_pad, (1, 1), (...]
    unnamed x3 -> x0, waiting for transfers between devices: 121 us -> none
    psum x1 -> x0, waiting for transfers between devices: 97.7 us -> none  [shards(): lax.psum((flat_grad, first_local), ('dp', 'space'))]
    concatenate x5 -> x2, local copies, waits for them, and re-layouts: 97.3 us -> 0.01 us  [shards(): jnp.concatenate(line, axis=2)]
    conv_general_dilated x16 -> x0, local copies, waits for them, and re-layouts: 72.2 us -> none  [the longest x6 42.1 us: strided(): lax.conv_general_dilated(inputs, kernel, (2, 2, 2), [(0, 0), (1, 1), (1,...]
    convert_element_type x10 -> x0, local copies, waits for them, and re-layouts: 61.8 us -> none  [the longest x6 42.1 us: shards(): hidden = leaky(preact_one).astype(jnp.bfloat16)]
    psum x1 -> x0, blocking collectives: 42.3 us -> none  [shards(): lax.psum((flat_grad, first_local), ('dp', 'space'))]
    concatenate x1 -> x2, other arithmetic: 32.8 us -> 0.9 us  [the longest x1 0.82 us: shards(): jnp.concatenate([jnp.concatenate(line, axis=2) for line in lines], axis=1)]
  transfers between devices with their start and end apart: 5 -> 3, of which waited for: 2 -> 2; matrix products, arithmetic and copies ran while one was open for 20% -> 6% of each run, Pallas kernels for 0% -> 0%
where the time goes in v1:
time: 71.9 us; the launch traced here: 71.3 us
  Pallas kernels  18.6 us (26%)
  waiting for transfers between devices  14.5 us (20%)
  starting transfers between devices  12.4 us (17%)
  blocking collectives  12.4 us (17%)
  local copies, waits for them, and re-layouts  9.85 us (14%)
  other arithmetic  2.79 us (4%)
  between operations  0.76 us (1%)
    pallas_call x2, Pallas kernels, call(): pl.pallas_call(kernel, out_shape=[jax.ShapeDtypeStruct(s, t) for s, t in...  18.6 us
    all_to_all x1, blocking collectives, gather(): return lax.all_to_all(wide, AXES, 0, 0, tiled=True)  12.4 us
    all_to_all x1, waiting for transfers between devices, scatter_sum(): return lax.all_to_all(values, AXES, 0, 0, tiled=True).sum(0)  9.67 us
    all_to_all x1, starting transfers between devices, scatter_sum(): return lax.all_to_all(values, AXES, 0, 0, tiled=True).sum(0)  8.73 us
    ppermute x2, waiting for transfers between devices, along(): lax.ppermute(value, axis, [(source, source + steps) for source in range(f...  4.87 us
    ppermute x2, starting transfers between devices, along(): lax.ppermute(value, axis, [(source, source + steps) for source in range(f...  3.66 us
  transfers between devices with their start and end apart: 3, of which 2 were waited for; matrix products, arithmetic and copies ran while one was open for 6% of the time, Pallas kernels for 0%

profile of v1, /device:TPU:0, one launch (start us, length us, event | category | flops | bytes accessed | tf_op | source)
XLA Modules:
  0.0 71.3 jit_solution(2909328899327647447)
XLA Ops:
  0.6 1.0 %slice_bitcast_fusion = bf16[4,3,32,512]{3,2,1,0:T(8,128)(2,1)S(1)} fusion(bf16[1,4,8,32,512]{4,3,2,1,0:T(8,128)(2,1)} %param.7), kind=kLoop, calls=%fused_computation.1 | loop fusion | bytes 786432 | tf_op jit(solution)/shard_map/squeeze | solution.py:191
  1.7 2.4 %collective-permute-start = (bf16[4,3,32,512]{3,2,1,0:T(8,128)(2,1)S(1)}, bf16[4,3,32,512]{3,2,1,0:T(8,128)(2,1)S(1)}, u32[]{:S(2)}, u32[]{:S(2)}) collective-permute-start(bf16[4,3,32,512]{3,2,1,0:T(8,128)(2,1)S(1)} %slice_bitcast_fusion), channel_id=1, source_target_pairs={{0,1},{1,2},{2,3},{3,4},{4,5},{5,6},{6,7},{8,9},{9,10},{10,11},{11... | collective-permute-start | bytes 1179656 | tf_op jit(solution)/shard_map/ppermute | solution.py:23
  4.1 1.0 %convert_element_type.3 = bf16[3,3,3,32,64]{4,3,2,1,0:T(8,128)(2,1)S(1)} convert(f32[3,3,3,32,64]{4,3,2,1,0:T(8,128)} %param.9) | non-fusion elementwise | flops 55296 | bytes 331776 | tf_op jit(solution)/shard_map/convert_element_type | solution.py:192
  5.1 0.8 %copy.30 = bf16[3,288,64]{1,2,0:T(8,128)(2,1)} copy(bf16[3,288,64]{2,1,0:T(8,128)(2,1)S(1)} %bitcast.49) | data formatting | bytes 221184 | tf_op jit(solution)/shard_map/reshape | solution.py:193
  5.9 1.4 %reshape.41.w1_ref = bf16[3,36,32]{2,1,0:T(8,128)(2,1)} reshape(bf16[3,3,3,4,32]{4,3,2,1,0:T(4,128)(2,1)} %param.8) | data formatting | bytes 13824 | tf_op jit(solution)/shard_map/reshape | solution.py:208
  7.4 0.0 collective-permute-done.vh_ref
  7.4 0.0 copy-start.1
  7.4 0.7 %copy-done.1 = bf16[4,3,32,512]{3,2,1,0:T(8,128)(2,1)} copy-done((bf16[4,3,32,512]{3,2,1,0:T(8,128)(2,1)}, bf16[4,3,32,512]{3,2,1,0:T(8,128)(2,1)S(1)}, u32[]{:S(2)}) %copy-start.1) | copy-done | bytes 393240
  8.1 12.0 %shard_map.110 = (bf16[64,2,8,128]{3,2,1,0:T(8,128)(2,1)}, bf16[11,1056,128]{2,1,0:T(8,128)(2,1)}, bf16[5,1632,128]{2,1,0:T(8,128)(2,1)}, bf16[2,1152,128]{2,1,0:T(8,128)(2,1)}, bf16[512,128]{1,0:T(8,128)(2,1)}) custom-call(bf16[4,8,32,512]{3,2,1,0:T(8,128)(2,1)} %bitcast.50, bf16[4,3,32,512]{3,2,1,0:T(8,128)(2,1)} %copy-done.1, ...), custom_call_target="tpu_custom_call" | custom-call | tf_op jit(solution)/shard_map/pallas_call | solution.py:170
  20.1 1.3 %collective-permute-start.1 = (bf16[512,128]{1,0:T(8,128)(2,1)}, bf16[512,128]{1,0:T(8,128)(2,1)S(1)}, u32[]{:S(2)}, u32[]{:S(2)}) collective-permute-start(bf16[512,128]{1,0:T(8,128)(2,1)} %get-tuple-element.16), channel_id=1, source_target_pairs={{1,0},{2,1},{3,2},{4,3},{5,4},{6,5},{7,6},{9,8},{10,9},{11,10},{12... | collective-permute-start | bytes 393224 | tf_op jit(solution)/shard_map/ppermute | solution.py:23
  21.4 0.8 %fusion.3 = bf16[3,128,256]{2,1,0:T(8,128)(2,1)} fusion(bf16[3,32,64]{2,1,0:T(8,128)(2,1)S(1)} %get-tuple-element.28, bf16[3,32,64]{2,1,0:T(8,128)(2,1)S(1)} %get-tuple-element.29, bf16[3,32,64]{2,1,0:T(8,128)(2,1)S(1)} %get-tuple-element.30, bf16[3,32,64]{2,1,0:T(8,128)(2,1)S(1)} %get-tuple-element.23, bf16[3,32,64]{2,1,0:T(8,128)(2,1)S(1)} %get-tuple-element.24, ...), kind=kLoop, calls=%fused_computation.7 | loop fusion | flops 2555904 | bytes 385024 | tf_op jit(solution)/shard_map/concatenate | solution.py:202
  22.2 4.9 %collective-permute-done.1.above_ref = bf16[512,128]{1,0:T(8,128)(2,1)S(1)} collective-permute-done((bf16[512,128]{1,0:T(8,128)(2,1)}, bf16[512,128]{1,0:T(8,128)(2,1)S(1)}, u32[]{:S(2)}, u32[]{:S(2)}) %collective-permute-start.1) | collective-permute-done | bytes 131104 | tf_op jit(solution)/shard_map/ppermute | solution.py:23
  27.1 0.6 copy-done.2
  27.7 6.6 %shard_map.111 = (f32[3,288,64]{2,1,0:T(8,128)}, f32[9,12,32]{2,1,0:T(8,128)}) custom-call(bf16[11,1056,128]{2,1,0:T(8,128)(2,1)} %get-tuple-element.13.d_ref, bf16[5,1632,128]{2,1,0:T(8,128)(2,1)} %get-tuple-element.14.h_ref, bf16[2,1152,128]{2,1,0:T(8,128)(2,1)} %get-tuple-element.15.d2_ref, bf16[512,128]{1,0:T(8,128)(2,1)} %copy-done.2, ...), custom_call_target="tpu_custom_call" | custom-call | tf_op jit(solution)/shard_map/pallas_call | solution.py:170
  34.4 1.2 %reshape.45 = f32[32,1728]{1,0:T(8,128)S(1)} reshape(f32[3,288,64]{2,1,0:T(8,128)} %get-tuple-element.17) | data formatting | bytes 442368 | tf_op jit(solution)/shard_map/reshape | solution.py:221
  35.5 1.0 %reshape.46 = f32[32,108]{1,0:T(8,128)S(1)} reshape(f32[9,12,32]{2,1,0:T(8,128)} %get-tuple-element.18) | data formatting | bytes 27648 | tf_op jit(solution)/shard_map/reshape | solution.py:220
  36.5 0.1 maximum_bitcast_fusion
  36.6 0.9 %copy.39 = f32[32,1,1836]{2,1,0:T(1,128)} copy(f32[32,1,1836]{2,0,1:T(8,128)S(1)} %maximum_bitcast_fusion) | data formatting | bytes 470016 | tf_op jit(solution)/shard_map/all_to_all | solution.py:181
  37.6 8.7 %all-to-all-start = ((f32[32,1,1836]{2,1,0:T(1,128)}), f32[32,1,1836]{2,1,0:T(1,128)S(1)}, u32[]{:S(2)}, u32[]{:S(2)}) async-start(f32[32,1,1836]{2,1,0:T(1,128)} %copy.39), calls=%async_computation | async-start | bytes 491520 | tf_op jit(solution)/shard_map/all_to_all | solution.py:181
  46.3 0.0 copy-done
  46.3 0.1 reshape.43
  46.4 9.7 %all-to-all-done = f32[32,1,1836]{2,1,0:T(1,128)S(1)} async-done(((f32[32,1,1836]{2,1,0:T(1,128)}), f32[32,1,1836]{2,1,0:T(1,128)S(1)}, u32[]{:S(2)}, u32[]{:S(2)}) %all-to-all-start) | async-done | bytes 235040 | tf_op jit(solution)/shard_map/all_to_all | solution.py:181
  56.1 0.2 reduce_sum.9
  56.3 0.1 slice.66
  56.4 0.0 copy-done.3
  56.4 0.6 divide_subtract_fusion
  57.0 0.1 pad_maximum_fusion
  57.0 0.1 broadcast_in_dim.14
  57.2 12.4 %all_to_all.18 = f32[32,1,1836]{2,1,0:T(1,128)S(1)} all-to-all(f32[32,1,1836]{2,1,0:T(1,128)S(1)} %broadcast_in_dim.14), channel_id=1, replica_groups=mesh['dp'=4,'space'=8] {'dp','space'}, dimensions={0} | all-to-all | bytes 470016 | tf_op jit(solution)/shard_map/all_to_all | solution.py:186
  69.6 0.1 slice.67
  69.7 0.9 %reshape.47 = f32[3,3,3,32,64]{4,3,2,1,0:T(8,128)} reshape(f32[32,1728]{1,0:T(8,128)S(1)} %slice.68) | data formatting | bytes 442368 | tf_op jit(solution)/shard_map/reshape | solution.py:229
  70.6 0.7 %reshape_reshape.3 = f32[3,3,3,4,32]{4,3,2,1,0:T(4,128)} reshape(f32[32,108]{1,0:T(8,128)S(1)} %slice.67) | data formatting | bytes 27648 | tf_op jit(solution)/shard_map/reshape;reshape | solution.py:230
  (11 shorter events, 0.1 us)
Async XLA Ops:
  1.7 5.7 %collective-permute-start = (bf16[4,3,32,512]{3,2,1,0:T(8,128)(2,1)S(1)}, bf16[4,3,32,512]{3,2,1,0:T(8,128)(2,1)S(1)}, u32[]{:S(2)}, u32[]{:S(2)}) collective-permute-start(bf16[4,3,32,512]{3,2,1,0:T(8,128)(2,1)S(1)} %slice_bitcast_fusion), channel_id=1, source_target_pairs={{0,1},{1,2},{2,3},{3,4},{4,5},{5,6},{6,7},{8,9},{9,10},{10,11},{11... | collective-permute-start | bytes 1179656 | tf_op jit(solution)/shard_map/ppermute | solution.py:23
  7.4 0.7 %copy-start.1 = (bf16[4,3,32,512]{3,2,1,0:T(8,128)(2,1)}, bf16[4,3,32,512]{3,2,1,0:T(8,128)(2,1)S(1)}, u32[]{:S(2)}) copy-start(bf16[4,3,32,512]{3,2,1,0:T(8,128)(2,1)S(1)} %collective-permute-done.vh_ref) | copy-start | bytes 1179652
  20.1 7.0 %collective-permute-start.1 = (bf16[512,128]{1,0:T(8,128)(2,1)}, bf16[512,128]{1,0:T(8,128)(2,1)S(1)}, u32[]{:S(2)}, u32[]{:S(2)}) collective-permute-start(bf16[512,128]{1,0:T(8,128)(2,1)} %get-tuple-element.16), channel_id=1, source_target_pairs={{1,0},{2,1},{3,2},{4,3},{5,4},{6,5},{7,6},{9,8},{10,9},{11,10},{12... | collective-permute-start | bytes 393224 | tf_op jit(solution)/shard_map/ppermute | solution.py:23
  27.1 0.7 copy-start.2
  27.7 18.6 %copy-start = (f32[3,3,3,32,64]{4,3,2,1,0:T(8,128)S(1)}, f32[3,3,3,32,64]{4,3,2,1,0:T(8,128)}, u32[]{:S(2)}) copy-start(f32[3,3,3,32,64]{4,3,2,1,0:T(8,128)} %param.9) | copy-start | bytes 663556
  34.3 22.0 %copy-start.3 = (f32[1728]{0:T(1024)S(1)}, f32[1728]{0:T(1024)}, u32[]{:S(2)}) copy-start(f32[1728]{0:T(1024)} %param.11) | copy-start | bytes 20740
  34.4 22.0 %copy-start.4 = (f32[1728]{0:T(1024)S(1)}, f32[1728]{0:T(1024)}, u32[]{:S(2)}) copy-start(f32[1728]{0:T(1024)} %param.12) | copy-start | bytes 20740
  37.6 18.6 %all-to-all-start = ((f32[32,1,1836]{2,1,0:T(1,128)}), f32[32,1,1836]{2,1,0:T(1,128)S(1)}, u32[]{:S(2)}, u32[]{:S(2)}) async-start(f32[32,1,1836]{2,1,0:T(1,128)} %copy.39), calls=%async_computation | async-start | bytes 491520 | tf_op jit(solution)/shard_map/all_to_all | solution.py:181

commit v2 on v1

v2 whole, which is shorter than its diff:
```python
import functools
import jax
import jax.numpy as jnp
import numpy as np
from jax import lax
from jax.experimental import pallas as pl
from jax.experimental.pallas import tpu as pltpu
from jax.sharding import PartitionSpec as P

SLOPE = 0.3
BETA_FIRST = 0.9
BETA_SECOND = 0.999
LEARN_RATE = 0.001
EPSILON = 1e-08
BF = jnp.bfloat16
F32 = jnp.float32
AXES = ("dp", "space")
LANES = 128


def along(value, axis, steps):
    count = lax.axis_size(axis)
    first, last = (max(0, -steps), min(count, count - steps))
    return lax.ppermute(value, axis, [(source, source + steps) for source in range(first, last)])


def leaky(values):
    return jnp.where(values > 0, values, SLOPE * values)


def nn(a, b):
    return lax.dot_general(a, b, (((1,), (0,)), ((), ())), preferred_element_type=F32)


def nt(a, b):
    return lax.dot_general(a, b, (((1,), (1,)), ((), ())), preferred_element_type=F32)


def tn(a, b):
    return lax.dot_general(a, b, (((0,), (0,)), ((), ())), preferred_element_type=F32)


def spread_taps():
    table = np.zeros((3, 3, 4, 2, 2, 256), np.float32)
    for dy in range(3):
        for dx in range(3):
            for c in range(4):
                for row in range(2):
                    for p in range(2):
                        table[dy, dx, c, row, p, (2 * row + dy) * 32 + (2 * p + dx) * 4 + c] = 1
    return table.reshape(36, 1024)


def repack(source, first, count, sel, stage, out, to):
    x = jnp.concatenate([source[:, first + i].reshape(4 * 32, 512) for i in range(count)], axis=0)
    lane = lax.broadcasted_iota(jnp.int32, (32, LANES), 1)
    for r in range(4):
        part = nn(x, sel[:, r * LANES:(r + 1) * LANES])
        for i in range(count):
            for c in range(4):
                block = part[i * 128 + c * 32:i * 128 + c * 32 + 32]
                stage[i, pl.ds(32 + (r + 1) * 4 + c, 32, stride=32), :] = block
                if r == 3:
                    moved = jnp.where(lane == 0, 0.0, pltpu.roll(block, 1, 1))
                    stage[i, pl.ds(32 + c, 32, stride=32), :] = moved
    for i in range(count):
        out[to + i] = stage[i].astype(BF)


def first_section(t1, planes, outs):
    lane = lax.broadcasted_iota(jnp.int32, (32, LANES), 1)
    for ref, z in outs:
        ref[z, 0:96] = jnp.zeros((96, LANES), BF)
    for m in range(8):
        acc = nn(t1[0], planes[0](m))
        acc += nn(t1[1], planes[1](m))
        acc += nn(t1[2], planes[2](m))
        both = leaky(acc)
        for k, (ref, z) in enumerate(outs):
            hid = both[:, k * LANES:(k + 1) * LANES]
            for i in range(2):
                at = (2 * m + i + 1) * 96
                odd = hid[i * 64 + 32:i * 64 + 64]
                ref[z, at:at + 32] = jnp.where(lane == 0, 0.0, pltpu.roll(odd, 1, 1)).astype(BF)
                ref[z, at + 32:at + 96] = hid[i * 64:i * 64 + 64].astype(BF)


def beside(*parts):
    return parts[0] if len(parts) == 1 else jnp.concatenate(parts, axis=1)


def pair_rows(*places):
    return lambda m: beside(*[ref[z, m * 128:m * 128 + 160] for ref, z in places])


def second_section(w2t, planes, cot_ref, z, rows_c, rows_a, put):
    lane = lax.broadcasted_iota(jnp.int32, (64, LANES), 1)
    rows_c[...] = cot_ref[:, z].astype(F32).reshape(512, LANES)
    for y in range(8):
        acc = nn(w2t[0], planes[0][0][planes[0][1], y * 192:y * 192 + 288])
        acc += nn(w2t[1], planes[1][0][planes[1][1], y * 192:y * 192 + 288])
        acc += nn(w2t[2], planes[2][0][planes[2][1], y * 192:y * 192 + 288])
        rows_a[pl.ds(y, 64, stride=8), :] = leaky(acc)
        delta = rows_c[pl.ds(y, 64, stride=8), :] * jnp.where(acc > 0, 1.0, SLOPE)
        left = jnp.where(lane == LANES - 1, 0.0, pltpu.roll(delta, LANES - 1, 1))
        put(y, delta.astype(BF), left.astype(BF))


def own_kernel(v_ref, w1_ref, e_ref, w2_ref, sel, t1, w2t, lmat, d_ref, h_ref, stage, w1s):
    lane = lax.broadcasted_iota(jnp.int32, (512, LANES), 1)
    row = lax.broadcasted_iota(jnp.int32, (512, LANES), 0)
    base = row - 4 * lane
    for r in range(4):
        sel[:, r * LANES:(r + 1) * LANES] = jnp.where(base == r, 1.0, 0.0).astype(BF)
    for j in range(27):
        w1s[j // 9, (j % 9) * 4:(j % 9) * 4 + 4, :] = w1_ref[j].astype(F32)
    for dz in range(3):
        taps = tn(w1s[dz, 0:36].astype(BF), e_ref[...]).astype(BF)
        for b in range(4):
            t1[dz, b * 32:(b + 1) * 32, :] = taps[:, b * 256:b * 256 + 160]
    eye = jnp.where(lax.broadcasted_iota(jnp.int32, (64, 64), 0) == lax.broadcasted_iota(jnp.int32, (64, 64), 1), 1.0, 0.0).astype(BF)
    step = lax.broadcasted_iota(jnp.int32, (64, LANES), 1) - lax.broadcasted_iota(jnp.int32, (64, LANES), 0)
    to_low = jnp.where(step == 0, 1.0, 0.0).astype(BF)
    to_high = jnp.where(step == 64, 1.0, 0.0).astype(BF)
    lmat[...] = jnp.zeros_like(lmat)
    for dz in range(3):
        w2 = w2_ref[dz].astype(BF)
        w2t[dz] = nt(eye, w2).astype(BF)
        low, high = nn(w2, to_low), nn(w2, to_high)
        tap = lambda half, dy, dx: half[(dy * 3 + dx) * 32:(dy * 3 + dx) * 32 + 32]
        at = dz * 128
        lmat[at:at + 32, 0:128] = tap(low, 1, 1).astype(BF)
        lmat[at + 32:at + 64, 0:128] = (tap(low, 1, 2) + tap(high, 1, 0)).astype(BF)
        lmat[at + 64:at + 96, 0:128] = tap(low, 2, 1).astype(BF)
        lmat[at + 96:at + 128, 0:128] = (tap(low, 2, 2) + tap(high, 2, 0)).astype(BF)
        lmat[at + 64:at + 96, 128:256] = tap(low, 0, 1).astype(BF)
        lmat[at + 96:at + 128, 128:256] = (tap(low, 0, 2) + tap(high, 0, 0)).astype(BF)
    stage[...] = jnp.zeros_like(stage)
    repack(v_ref, 0, 4, sel, stage, d_ref, 0)
    repack(v_ref, 4, 4, sel, stage, d_ref, 4)
    first_section(t1, [pair_rows((d_ref, 1 + dz), (d_ref, 3 + dz)) for dz in range(3)], [(h_ref, 0), (h_ref, 1)])
    first_section(t1, [pair_rows((d_ref, 5 + dz)) for dz in range(3)], [(h_ref, 2)])


def halo_kernel(vh_ref, cot_ref, sel, t1, w2t, d_ref, h_ref, dl_ref, hl_ref, d2_ref, edge_ref, a0_ref, stage, rows_c, rows_a):
    stage[...] = jnp.zeros_like(stage)
    repack(vh_ref, 0, 3, sel, stage, dl_ref, 0)
    first_section(t1, [pair_rows((dl_ref, 0), (dl_ref, 2)), pair_rows((dl_ref, 1), (d_ref, 0)), pair_rows((dl_ref, 2), (d_ref, 1))],
                  [(hl_ref, 0), (hl_ref, 1)])
    d2_ref[1024:1152] = jnp.zeros((128, LANES), BF)

    def put(y, delta, left):
        d2_ref[y * 128:y * 128 + 64] = delta
        d2_ref[y * 128 + 64:y * 128 + 128] = left
        edge_ref[y * 64:y * 64 + 64] = delta

    second_section(w2t, [(hl_ref, 0), (hl_ref, 1), (h_ref, 0)], cot_ref, 0, rows_c, rows_a, put)
    a0_ref[...] = rows_a[...].astype(BF).reshape(64, 8, LANES)


def slopes(ref, z, m):
    parts = [jnp.where(ref[z, (2 * m + i + 1) * 96 + 32:(2 * m + i + 1) * 96 + 96].astype(F32) > 0, 1.0, SLOPE) for i in range(2)]
    return jnp.concatenate(parts, axis=0)


def inner_kernel(cot_ref, w2t, lmat, d_ref, h_ref, dl_ref, hl_ref, d2_ref, a0_ref,
                 act_ref, g2_ref, g1_ref, grad_ref, d2n, d1, rows_c, rows_a):
    d2n[1024:1152] = jnp.zeros((128, LANES), BF)

    def put(y, delta, left):
        d2n[y * 128:y * 128 + 64] = delta
        d2n[y * 128 + 64:y * 128 + 128] = left

    second_section(w2t, [(h_ref, 0), (h_ref, 1), (h_ref, 2)], cot_ref, 1, rows_c, rows_a, put)
    act_ref[:, 0] = a0_ref[...]
    act_ref[:, 1] = rows_a[...].astype(BF).reshape(64, 8, LANES)
    lower = [(hl_ref, 0), (hl_ref, 1), (h_ref, 0)]
    for dz in range(3):
        acc = jnp.zeros((288, LANES), F32)
        ref, z = lower[dz]
        for y in range(8):
            a = beside(ref[z, y * 192:y * 192 + 288], h_ref[dz, y * 192:y * 192 + 288])
            b = beside(d2_ref[y * 128:y * 128 + 128], d2n[y * 128:y * 128 + 128])
            acc += nt(a, b)
        g2_ref[dz * 288:dz * 288 + 288] = acc
    g2_ref[864:872] = jnp.zeros((8, LANES), F32)
    for m in range(8):
        rows = slice(m * 128, m * 128 + 128)
        r0 = nn(lmat[128:384], d2_ref[m * 128:m * 128 + 256])
        r1 = nn(lmat[...], d2n[m * 128:m * 128 + 256])
        d1[0, rows] = (r0[0:128] * slopes(hl_ref, 1, m)).astype(BF)
        d1[1, rows] = ((r0[128:256] + r1[0:128]) * slopes(h_ref, 0, m)).astype(BF)
        d1[2, rows] = (r1[128:256] * slopes(h_ref, 1, m)).astype(BF)
        grad_ref[rows] = r1[256:384]
    lower = [(dl_ref, 2), (d_ref, 0), (d_ref, 1)]
    for dz in range(3):
        acc = jnp.zeros((128, 160), F32)
        two, one = pair_rows(lower[dz], (d_ref, 1 + dz)), pair_rows((d_ref, 3 + dz))
        for m in range(8):
            rows = slice(m * 128, m * 128 + 128)
            acc += nt(beside(d1[0, rows], d1[1, rows]), two(m))
            acc += nt(d1[2, rows], one(m))
        g1_ref[dz] = acc


def edge_kernel(share, packed, above_ref, lmat, d_ref, h_ref, g2_ref, g1_ref, grad_ref, out_ref, d2h, d1):
    lane = lax.broadcasted_iota(jnp.int32, (64, LANES), 1)
    d2h[1024:1152] = jnp.zeros((128, LANES), BF)
    for y in range(8):
        low = above_ref[y * 64:y * 64 + 64]
        left = jnp.where(lane == LANES - 1, 0.0, pltpu.roll(low.astype(F32), LANES - 1, 1))
        d2h[y * 128:y * 128 + 64] = low
        d2h[y * 128 + 64:y * 128 + 128] = left.astype(BF)
    for m in range(8):
        rows = slice(m * 128, m * 128 + 128)
        grad = grad_ref[rows] + nn(lmat[0:128], d2h[m * 128:m * 128 + 256])
        d1[rows] = (grad * slopes(h_ref, 2, m)).astype(BF)
    lane = lax.broadcasted_iota(jnp.int32, (32, LANES), 1)
    total = jnp.zeros((32, LANES), F32)
    for dz in range(3):
        acc = g1_ref[dz]
        rows_of = pair_rows((d_ref, 5 + dz))
        for m in range(8):
            acc += nt(d1[m * 128:m * 128 + 128], rows_of(m))
        wide = (acc[:, 0:128], jnp.concatenate([acc[:, 128:160], jnp.zeros((128, 96), F32)], axis=1))
        for dy in range(3):
            to = (dz * 3 + dy) * 12
            part = jnp.zeros((32, LANES), F32)
            for i in range(2):
                for p in range(2):
                    y = 2 * i + dy
                    block = wide[y // 4][(2 * i + p) * 32:(2 * i + p) * 32 + 32]
                    shift = (to - ((y % 4) * 32 + 8 * p)) % LANES
                    part += block if shift == 0 else pltpu.roll(block, shift, 1)
            total = jnp.where((lane >= to) & (lane < to + 12), part, total)
    if not packed:
        out_ref[...] = total
        return
    count = share // 64
    low = lax.broadcasted_iota(jnp.int32, (14, LANES), 1) < 64
    for k in range(32):
        even = g2_ref[pl.ds(count * k, 14, stride=2), :]
        odd = g2_ref[pl.ds(count * k + 1, 14, stride=2), :]
        out_ref[k, 0:14] = jnp.where(low, even, pltpu.roll(odd, 64, 1))
        out_ref[k, 14:15] = total[k:k + 1]
        out_ref[k, 15:16] = jnp.zeros((1, LANES), F32)


def spread_kernel(count, full_ref, kernel_ref, first_ref, lines):
    for k in range(32):
        x = full_ref[k]
        lines[pl.ds(count * k, 14, stride=2), :] = x[0:14]
        lines[pl.ds(count * k + 1, 13, stride=2), :] = pltpu.roll(x, 64, 1)[0:13]
    kernel_ref[...] = lines[0:864, 0:64]
    columns = jnp.concatenate([full_ref[k, 14:15] for k in range(32)] + [jnp.zeros((96, LANES), F32)], axis=0)
    turned = columns.T
    for j in range(27):
        first_ref[j] = turned[j * 4:j * 4 + 4, 0:32]


VMEM = pl.BlockSpec(memory_space=pltpu.VMEM)


def call(kernel, outs, scratch, args):
    return pl.pallas_call(
        kernel,
        out_shape=[pltpu.VMEM(s, t) if stays else jax.ShapeDtypeStruct(s, t) for s, t, stays in outs],
        in_specs=[VMEM] * len(args),
        out_specs=[VMEM] * len(outs),
        scratch_shapes=[pltpu.VMEM(s, t) for s, t in scratch],
        compiler_params=pltpu.CompilerParams(vmem_limit_bytes=40 * 1024 * 1024),
    )(*args)


def stay(*arrays):
    return [pltpu.with_memory_space_constraint(a, pltpu.VMEM) for a in arrays]


def gather(values, count):
    wide = jnp.broadcast_to(values[None], (count,) + values.shape)
    return lax.all_to_all(wide, AXES, 0, 0, tiled=True)


def shards(volumes, first_kernel, second_kernel, cotangent, first_moment, second_moment):
    count = lax.axis_size(AXES)
    share = first_moment.shape[0]
    packed = count == 32 and share == 1728
    below = along(volumes[0, :, -3:], "space", 1)
    deep = lambda n: ((n, 1056, LANES), BF, True)
    hidden = lambda n: ((n, 1632, LANES), BF, True)
    sel, t1, w2t, lmat, d, h = call(
        own_kernel,
        [((512, 512), BF, True), ((3, 128, 160), BF, True), ((3, 64, 288), BF, True), ((384, 256), BF, True), deep(8), hidden(3)],
        [((4, 1056, LANES), F32), ((3, 40, 32), F32)],
        (volumes[0], first_kernel.reshape(27, 4, 32), jnp.asarray(spread_taps(), BF), second_kernel.reshape(3, 288, 64)),
    )
    sel, t1, w2t, lmat, d, h = stay(sel, t1, w2t, lmat, d, h)
    dl, hl, d2, edge, a0 = call(
        halo_kernel,
        [deep(3), hidden(2), ((1152, LANES), BF, True), ((512, LANES), BF, False), ((64, 8, LANES), BF, True)],
        [((3, 1056, LANES), F32), ((512, LANES), F32), ((512, LANES), F32)],
        (below, cotangent[0], sel, t1, w2t, d, h),
    )
    above = along(edge, "space", -1)
    dl, hl, d2, a0 = stay(dl, hl, d2, a0)
    act, g2, g1, grad = call(
        inner_kernel,
        [((64, 2, 8, LANES), BF, False), ((872, LANES), F32, packed), ((3, 128, 160), F32, True), ((1024, LANES), F32, True)],
        [((1152, LANES), BF), ((3, 1024, LANES), BF), ((512, LANES), F32), ((512, LANES), F32)],
        (cotangent[0], w2t, lmat, d, h, dl, hl, d2, a0),
    )
    g1, grad = stay(g1, grad)
    if packed:
        (g2,) = stay(g2)
    (out,) = call(
        functools.partial(edge_kernel, share, packed),
        [((32, 16, LANES) if packed else (32, LANES), F32, False)],
        [((1152, LANES), BF), ((1024, LANES), BF)],
        (above, lmat, d, h, g2, g1, grad),
    )
    if packed:
        both = lax.all_to_all(out, AXES, 0, 0, tiled=True).sum(0).reshape(-1)
    else:
        one = out[:, :108].T.reshape(-1)
        one = jnp.pad(one, (0, -one.shape[0] % count)).reshape(count, -1)
        both = jnp.concatenate([g2[:864, :64].reshape(count, share), one], axis=1)
        both = lax.all_to_all(both, AXES, 0, 0, tiled=True).sum(0)
    grad_share = both[:share]
    offset = lax.axis_index(AXES) * share
    new_first = BETA_FIRST * first_moment + (1.0 - BETA_FIRST) * grad_share
    new_second = BETA_SECOND * second_moment + (1.0 - BETA_SECOND) * grad_share * grad_share
    kernel_share = lax.dynamic_slice_in_dim(second_kernel.reshape(-1), offset, share, 0)
    updated = kernel_share - LEARN_RATE * new_first / (jnp.sqrt(new_second) + EPSILON)
    send = jnp.concatenate([updated, both[share:]])
    if packed:
        full = gather(send.reshape(16, LANES), count)
        new_kernel, first_gradient = call(
            functools.partial(spread_kernel, share // 64),
            [((864, 64), F32, False), ((27, 4, 32), F32, False)], [((880, LANES), F32)], (full,))
    else:
        full = gather(send, count)
        new_kernel = full[:, :share]
        first_gradient = full[:, share:].reshape(-1)[:first_kernel.size]
    return (act[None], first_gradient.reshape(first_kernel.shape), new_kernel.reshape(second_kernel.shape), new_first, new_second)


def solution(mesh):
    field = P("dp", None, "space", None, None)
    flat = P(AXES)
    return jax.shard_map(
        shards, mesh=mesh, in_specs=(field, P(), P(), field, flat, flat),
        out_specs=(field, P(), P(), flat, flat), check_vma=False)
```

time: 71.9 us -> 55.8 us (0.78)
  Pallas kernels: 18.6 us -> 13 us
  local copies, waits for them, and re-layouts: 9.85 us -> 5.16 us
  waiting for transfers between devices: 14.5 us -> 10.3 us
  other arithmetic: 2.79 us -> 0.72 us
    pallas_call x2 -> x5, Pallas kernels: 18.6 us -> 13 us  [call(): pl.pallas_call(kernel, out_shape=[pltpu.VMEM(s, t) if stays else jax.Shap...]
    reshape x5 -> x0, local copies, waits for them, and re-layouts: 5.27 us -> none  [the longest x1 1.38 us: shards(): first_kernel.reshape(3, 36, 32)]
    ppermute x2, waiting for transfers between devices: 4.87 us -> 0.07 us  [along(): lax.ppermute(value, axis, [(source, source + steps) for source in range(f...]
    unnamed x11 -> x16, local copies, waits for them, and re-layouts: 1.42 us -> 3.88 us
    convert_element_type x1 -> x0, other arithmetic: 1.05 us -> none  [shards(): kernel_half = second_kernel.astype(BF)]
    all_to_all x1 -> x0, local copies, waits for them, and re-layouts: 0.95 us -> none  [scatter_sum(): return lax.all_to_all(values, AXES, 0, 0, tiled=True).sum(0)]
    concatenate x2 -> x0, other arithmetic: 0.9 us -> none  [the longest x1 0.82 us: shards(): jnp.concatenate([jnp.concatenate(line, axis=2) for line in lines], axis=1)]
    another operation x1 -> x0, local copies, waits for them, and re-layouts: 0.74 us -> none  [shards(): full[:, share:].reshape(-1)[:first_kernel.size].reshape(first_kernel.shape)]
  transfers between devices with their start and end apart: 3 -> 3, of which waited for: 2 -> 2; matrix products, arithmetic and copies ran while one was open for 6% -> 0% of each run, Pallas kernels for 0% -> 15%
where the time goes in v2:
time: 55.8 us; the launch traced here: 55.4 us
  Pallas kernels  13 us (23%)
  starting transfers between devices  12.8 us (23%)
  blocking collectives  12.7 us (23%)
  waiting for transfers between devices  10.3 us (18%)
  local copies, waits for them, and re-layouts  5.16 us (9%)
  between operations  0.73 us (1%)
  other arithmetic  0.72 us (1%)
    pallas_call x5, Pallas kernels, call(): pl.pallas_call(kernel, out_shape=[pltpu.VMEM(s, t) if stays else jax.Shap...  13 us
    all_to_all x1, blocking collectives, gather(): return lax.all_to_all(wide, AXES, 0, 0, tiled=True)  12.7 us
    all_to_all x1, waiting for transfers between devices, shards(): both = lax.all_to_all(out, AXES, 0, 0, tiled=True).sum(0).reshape(-1)  10.2 us
    all_to_all x1, starting transfers between devices, shards(): both = lax.all_to_all(out, AXES, 0, 0, tiled=True).sum(0).reshape(-1)  9.12 us
    unnamed x16, local copies, waits for them, and re-layouts  3.88 us
    ppermute x2, starting transfers between devices, along(): lax.ppermute(value, axis, [(source, source + steps) for source in range(f...  3.67 us
  transfers between devices with their start and end apart: 3, of which 2 were waited for; matrix products, arithmetic and copies ran while one was open for 0% of the time, Pallas kernels for 15%

profile of v2, /device:TPU:0, one launch (start us, length us, event | category | flops | bytes accessed | tf_op | source)
XLA Modules:
  0.0 55.4 jit_solution(5660944866605882295)
XLA Ops:
  0.6 0.0 copy-start.3
  0.6 1.1 %slice_bitcast_fusion = bf16[4,3,32,512]{3,2,1,0:T(8,128)(2,1)S(1)} fusion(bf16[1,4,8,32,512]{4,3,2,1,0:T(8,128)(2,1)} %param.7), kind=kLoop, calls=%fused_computation | loop fusion | bytes 786432 | tf_op jit(solution)/shard_map/squeeze | solution.py:288
  1.7 2.4 %collective-permute-start = (bf16[4,3,32,512]{3,2,1,0:T(8,128)(2,1)S(1)}, bf16[4,3,32,512]{3,2,1,0:T(8,128)(2,1)S(1)}, u32[]{:S(2)}, u32[]{:S(2)}) collective-permute-start(bf16[4,3,32,512]{3,2,1,0:T(8,128)(2,1)S(1)} %slice_bitcast_fusion), channel_id=1, source_target_pairs={{0,1},{1,2},{2,3},{3,4},{4,5},{5,6},{6,7},{8,9},{9,10},{10,11},{11... | collective-permute-start | bytes 1179656 | tf_op jit(solution)/shard_map/ppermute | solution.py:24
  4.1 0.0 copy-start
  4.1 1.2 %copy-done = bf16[1,4,8,32,512]{4,3,2,1,0:T(8,128)(2,1)S(1)} copy-done((bf16[1,4,8,32,512]{4,3,2,1,0:T(8,128)(2,1)S(1)}, bf16[1,4,8,32,512]{4,3,2,1,0:T(8,128)(2,1)}, u32[]{:S(2)}) %copy-start) | copy-done | bytes 1048600
  5.3 0.0 copy-start.1
  5.3 1.0 %copy-done.1 = f32[3,3,3,32,64]{4,3,2,1,0:T(8,128)S(1)} copy-done((f32[3,3,3,32,64]{4,3,2,1,0:T(8,128)S(1)}, f32[3,3,3,32,64]{4,3,2,1,0:T(8,128)}, u32[]{:S(2)}) %copy-start.1) | copy-done | bytes 221208
  6.3 0.0 copy-start.4
  6.3 0.9 %copy-done.4 = bf16[36,1024]{1,0:T(8,128)(2,1)S(1)} copy-done((bf16[36,1024]{1,0:T(8,128)(2,1)S(1)}, bf16[36,1024]{1,0:T(8,128)(2,1)}, u32[]{:S(2)}) %copy-start.4) | copy-done | bytes 73752
  7.2 0.0 copy-start.5
  7.2 0.7 %copy-done.5 = bf16[3,3,3,4,32]{4,3,2,1,0:T(4,128)(2,1)S(1)} copy-done((bf16[3,3,3,4,32]{4,3,2,1,0:T(4,128)(2,1)S(1)}, bf16[3,3,3,4,32]{4,3,2,1,0:T(4,128)(2,1)}, u32[]{:S(2)}) %copy-start.5) | copy-done | bytes 6936
  8.0 4.1 %shard_map.110 = (bf16[512,512]{1,0:T(8,128)(2,1)S(1)}, bf16[3,128,160]{2,1,0:T(8,128)(2,1)S(1)}, bf16[3,64,288]{2,1,0:T(8,128)(2,1)S(1)}, bf16[384,256]{1,0:T(8...) custom-call(bf16[4,8,32,512]{3,2,1,0:T(8,128)(2,1)S(1)} %bitcast.14, ...), custom_call_target="tpu_custom_call" | custom-call | tf_op jit(solution)/shard_map/pallas_call | solution.py:265
  12.1 0.0 collective-permute-done.vh_ref
  12.1 0.0 copy-done.3
  12.1 2.1 %shard_map.111 = (bf16[3,1056,128]{2,1,0:T(8,128)(2,1)S(1)}, bf16[2,1632,128]{2,1,0:T(8,128)(2,1)S(1)}, bf16[1152,128]{1,0:T(8,128)(2,1)S(1)}, bf16[512,128]{1,0:T(8,128)(2,1)S(1)}, bf16[64,8,128]{2,1,0:T(8,128)(2,1)S(1)}) custom-call(bf16[4,3,32,512]{3,2,1,0:T(8,128)(2,1)S(1)} %collective-permute-done.vh_ref, bf16[64,2,8,128]{3,2,1,0:T(8,128)(2,1)S(1)} %bitcast.16, ...), custom_call_target="tpu_custom_call" | custom-call | tf_op jit(solution)/shard_map/pallas_call | solution.py:265
  14.2 1.3 %collective-permute-start.1 = (bf16[512,128]{1,0:T(8,128)(2,1)S(1)}, bf16[512,128]{1,0:T(8,128)(2,1)S(1)}, u32[]{:S(2)}, u32[]{:S(2)}) collective-permute-start(bf16[512,128]{1,0:T(8,128)(2,1)S(1)} %get-tuple-element.33), channel_id=1, source_target_pairs={{1,0},{2,1},{3,2},{4,3},{5,4},{6,5},{7,6},{9,8},{10,9},{11,10},{12... | collective-permute-start | bytes 393224 | tf_op jit(solution)/shard_map/ppermute | solution.py:24
  15.5 4.0 %shard_map.112 = (bf16[64,2,8,128]{3,2,1,0:T(8,128)(2,1)}, f32[872,128]{1,0:T(8,128)S(1)}, f32[3,128,160]{2,1,0:T(8,128)S(1)}, f32[1024,128]{1,0:T(8,128)S(1)}) custom-call(bf16[64,2,8,128]{3,2,1,0:T(8,128)(2,1)S(1)} %bitcast.17, bf16[3,64,288]{2,1,0:T(8,128)(2,1)S(1)} %get-tuple-element.22.w2t, bf16[384,256]{1,0:T(8,128)(2,1)S(1)} %get-tuple-element.23.lmat, ...), custom_call_target="tpu_custom_call" | custom-call | tf_op jit(solution)/shard_map/pallas_call | solution.py:265
  19.5 0.1 collective-permute-done.1.above_ref
  19.6 0.0 copy-start.2
  19.6 0.0 copy-start.6
  19.6 1.8 %shard_map.113 = f32[32,16,128]{2,1,0:T(8,128)} custom-call(bf16[512,128]{1,0:T(8,128)(2,1)S(1)} %collective-permute-done.1.above_ref, bf16[384,256]{1,0:T(8,128)(2,1)S(1)} %get-tuple-element.23.lmat, bf16[8,1056,128]{2,1,0:T(8,128)(2,1)S(1)} %get-tuple-element.24.d_ref, bf16[3,1632,128]{2,1,0:T(8,128)(2,1)S(1)} %get-tuple-element.25.h_ref, ...), custom_call_target="tpu_custom_call" | custom-call | tf_op jit(solution)/shard_map/pallas_call | solution.py:265
  21.4 9.1 %all-to-all-start = ((f32[32,16,128]{2,1,0:T(8,128)}), f32[32,16,128]{2,1,0:T(8,128)S(1)}, u32[]{:S(2)}, u32[]{:S(2)}) async-start(f32[32,16,128]{2,1,0:T(8,128)} %shard_map.113), calls=%async_computation | async-start | bytes 524288 | tf_op jit(solution)/shard_map/all_to_all | solution.py:322
  30.5 0.0 copy-done.2
  30.5 0.1 reshape.31
  30.7 10.2 %all-to-all-done = f32[32,16,128]{2,1,0:T(8,128)S(1)} async-done(((f32[32,16,128]{2,1,0:T(8,128)}), f32[32,16,128]{2,1,0:T(8,128)S(1)}, u32[]{:S(2)}, u32[]{:S(2)}) %all-to-all-start) | async-done | bytes 262176 | tf_op jit(solution)/shard_map/all_to_all | solution.py:322
  40.9 0.1 slice.13
  41.0 0.0 copy-done.6
  41.0 0.0 copy-done.7
  41.0 0.6 %divide_subtract_fusion = (f32[1728]{0:T(1024)S(1)}, f32[1728]{0:T(1024)}, f32[1728]{0:T(1024)}) fusion(f32[55296]{0:T(1024)S(1)} %reshape.31, s32[]{:T(128)S(6)} %select_n.3, f32[2048]{0:T(1024)S(1)} %bitcast.20, f32[1728]{0:T(1024)S(1)} %copy-done.6, f32[1728]{0:T(1024)S(1)} %copy-done.7), kind=kLoop, calls=%fused_computation.4 | loop fusion | flops 19008 | bytes 48388 | tf_op jit(solution)/shard_map/sub | solution.py:333
  41.6 0.1 maximum_bitcast_fusion
  41.7 12.7 %all_to_all.10.full_ref = f32[32,16,128]{2,1,0:T(8,128)S(1)} all-to-all(f32[32,16,128]{2,1,0:T(8,128)S(1)} %broadcast_in_dim.12), channel_id=1, replica_groups=mesh['dp'=4,'space'=8] {'dp','space'}, dimensions={0} | all-to-all | bytes 524288 | tf_op jit(solution)/shard_map/all_to_all | solution.py:281
  54.4 0.9 %shard_map.114 = (f32[864,64]{1,0:T(8,128)}, f32[27,4,32]{2,1,0:T(4,128)}) custom-call(f32[32,16,128]{2,1,0:T(8,128)S(1)} %all_to_all.10.full_ref), custom_call_target="tpu_custom_call" | custom-call | tf_op jit(solution)/shard_map/pallas_call | solution.py:265
  (3 shorter events, 0.1 us)
Async XLA Ops:
  0.6 11.5 %copy-start.3 = (bf16[1,64,2,8,128]{4,3,2,1,0:T(8,128)(2,1)S(1)}, bf16[1,64,2,8,128]{4,3,2,1,0:T(8,128)(2,1)}, u32[]{:S(2)}) copy-start(bf16[1,64,2,8,128]{4,3,2,1,0:T(8,128)(2,1)} %param.10) | copy-start | bytes 786436
  1.7 10.4 %collective-permute-start = (bf16[4,3,32,512]{3,2,1,0:T(8,128)(2,1)S(1)}, bf16[4,3,32,512]{3,2,1,0:T(8,128)(2,1)S(1)}, u32[]{:S(2)}, u32[]{:S(2)}) collective-permute-start(bf16[4,3,32,512]{3,2,1,0:T(8,128)(2,1)S(1)} %slice_bitcast_fusion), channel_id=1, source_target_pairs={{0,1},{1,2},{2,3},{3,4},{4,5},{5,6},{6,7},{8,9},{9,10},{10,11},{11... | collective-permute-start | bytes 1179656 | tf_op jit(solution)/shard_map/ppermute | solution.py:24
  4.1 1.2 %copy-start = (bf16[1,4,8,32,512]{4,3,2,1,0:T(8,128)(2,1)S(1)}, bf16[1,4,8,32,512]{4,3,2,1,0:T(8,128)(2,1)}, u32[]{:S(2)}) copy-start(bf16[1,4,8,32,512]{4,3,2,1,0:T(8,128)(2,1)} %param.7) | copy-start | bytes 3145732
  5.3 1.0 %copy-start.1 = (f32[3,3,3,32,64]{4,3,2,1,0:T(8,128)S(1)}, f32[3,3,3,32,64]{4,3,2,1,0:T(8,128)}, u32[]{:S(2)}) copy-start(f32[3,3,3,32,64]{4,3,2,1,0:T(8,128)} %param.9) | copy-start | bytes 663556
  6.3 0.9 %copy-start.4 = (bf16[36,1024]{1,0:T(8,128)(2,1)S(1)}, bf16[36,1024]{1,0:T(8,128)(2,1)}, u32[]{:S(2)}) copy-start(bf16[36,1024]{1,0:T(8,128)(2,1)} %constant.30.clone.e_ref) | copy-start | bytes 221188
  7.2 0.7 %copy-start.5 = (bf16[3,3,3,4,32]{4,3,2,1,0:T(4,128)(2,1)S(1)}, bf16[3,3,3,4,32]{4,3,2,1,0:T(4,128)(2,1)}, u32[]{:S(2)}) copy-start(bf16[3,3,3,4,32]{4,3,2,1,0:T(4,128)(2,1)} %param.8) | copy-start | bytes 20740
  14.2 5.4 %collective-permute-start.1 = (bf16[512,128]{1,0:T(8,128)(2,1)S(1)}, bf16[512,128]{1,0:T(8,128)(2,1)S(1)}, u32[]{:S(2)}, u32[]{:S(2)}) collective-permute-start(bf16[512,128]{1,0:T(8,128)(2,1)S(1)} %get-tuple-element.33), channel_id=1, source_target_pairs={{1,0},{2,1},{3,2},{4,3},{5,4},{6,5},{7,6},{9,8},{10,9},{11,10},{12... | collective-permute-start | bytes 393224 | tf_op jit(solution)/shard_map/ppermute | solution.py:24
  19.6 10.9 %copy-start.2 = (f32[3,3,3,32,64]{4,3,2,1,0:T(8,128)S(1)}, f32[3,3,3,32,64]{4,3,2,1,0:T(8,128)}, u32[]{:S(2)}) copy-start(f32[3,3,3,32,64]{4,3,2,1,0:T(8,128)} %param.9) | copy-start | bytes 663556
  19.6 21.4 %copy-start.6 = (f32[1728]{0:T(1024)S(1)}, f32[1728]{0:T(1024)}, u32[]{:S(2)}) copy-start(f32[1728]{0:T(1024)} %param.11) | copy-start | bytes 20740
  19.6 21.4 %copy-start.7 = (f32[1728]{0:T(1024)S(1)}, f32[1728]{0:T(1024)}, u32[]{:S(2)}) copy-start(f32[1728]{0:T(1024)} %param.12) | copy-start | bytes 20740
  21.4 19.5 %all-to-all-start = ((f32[32,16,128]{2,1,0:T(8,128)}), f32[32,16,128]{2,1,0:T(8,128)S(1)}, u32[]{:S(2)}, u32[]{:S(2)}) async-start(f32[32,16,128]{2,1,0:T(8,128)} %shard_map.113), calls=%async_computation | async-start | bytes 524288 | tf_op jit(solution)/shard_map/all_to_all | solution.py:322

commit v3 on v2

--- a/solution.py
+++ b/solution.py
@@ -106,12 +106,21 @@
         put(y, delta.astype(BF), left.astype(BF))
 
 
-def own_kernel(v_ref, w1_ref, e_ref, w2_ref, sel, t1, w2t, lmat, d_ref, h_ref, stage, w1s):
+def own_kernel(v_hbm, w1_hbm, e_hbm, w2_hbm, cot_hbm, sel, t1, w2t, lmat, d_ref, h_ref, cot_ref,
+               stage, w1s, v_ref, w1_ref, e_ref, w2_ref, sems):
+    moves = [pltpu.make_async_copy(source, target, sems.at[i]) for i, (source, target) in enumerate((
+        (w1_hbm, w1_ref), (e_hbm, e_ref), (w2_hbm, w2_ref),
+        (v_hbm.at[:, 0:4], v_ref.at[:, 0:4]), (v_hbm.at[:, 4:8], v_ref.at[:, 4:8]), (cot_hbm, cot_ref)))]
+    for move in moves:
+        move.start()
     lane = lax.broadcasted_iota(jnp.int32, (512, LANES), 1)
     row = lax.broadcasted_iota(jnp.int32, (512, LANES), 0)
     base = row - 4 * lane
     for r in range(4):
         sel[:, r * LANES:(r + 1) * LANES] = jnp.where(base == r, 1.0, 0.0).astype(BF)
+    stage[...] = jnp.zeros_like(stage)
+    moves[0].wait()
+    moves[1].wait()
     for j in range(27):
         w1s[j // 9, (j % 9) * 4:(j % 9) * 4 + 4, :] = w1_ref[j].astype(F32)
     for dz in range(3):
@@ -123,6 +132,7 @@
     to_low = jnp.where(step == 0, 1.0, 0.0).astype(BF)
     to_high = jnp.where(step == 64, 1.0, 0.0).astype(BF)
     lmat[...] = jnp.zeros_like(lmat)
+    moves[2].wait()
     for dz in range(3):
         w2 = w2_ref[dz].astype(BF)
         w2t[dz] = nt(eye, w2).astype(BF)
@@ -135,11 +145,13 @@
         lmat[at + 96:at + 128, 0:128] = (tap(low, 2, 2) + tap(high, 2, 0)).astype(BF)
         lmat[at + 64:at + 96, 128:256] = tap(low, 0, 1).astype(BF)
         lmat[at + 96:at + 128, 128:256] = (tap(low, 0, 2) + tap(high, 0, 0)).astype(BF)
-    stage[...] = jnp.zeros_like(stage)
+    moves[3].wait()
     repack(v_ref, 0, 4, sel, stage, d_ref, 0)
+    moves[4].wait()
     repack(v_ref, 4, 4, sel, stage, d_ref, 4)
     first_section(t1, [pair_rows((d_ref, 1 + dz), (d_ref, 3 + dz)) for dz in range(3)], [(h_ref, 0), (h_ref, 1)])
     first_section(t1, [pair_rows((d_ref, 5 + dz)) for dz in range(3)], [(h_ref, 2)])
+    moves[5].wait()
 
 
 def halo_kernel(vh_ref, cot_ref, sel, t1, w2t, d_ref, h_ref, dl_ref, hl_ref, d2_ref, edge_ref, a0_ref, stage, rows_c, rows_a):
@@ -163,8 +175,8 @@
     return jnp.concatenate(parts, axis=0)
 
 
-def inner_kernel(cot_ref, w2t, lmat, d_ref, h_ref, dl_ref, hl_ref, d2_ref, a0_ref,
-                 act_ref, g2_ref, g1_ref, grad_ref, d2n, d1, rows_c, rows_a):
+def inner_kernel(share, packed, cot_ref, w2t, lmat, d_ref, h_ref, dl_ref, hl_ref, d2_ref, a0_ref,
+                 act_ref, out_ref, g1_ref, grad_ref, g2_ref, d2n, d1, rows_c, rows_a):
     d2n[1024:1152] = jnp.zeros((128, LANES), BF)
 
     def put(y, delta, left):
@@ -184,6 +196,15 @@
             acc += nt(a, b)
         g2_ref[dz * 288:dz * 288 + 288] = acc
     g2_ref[864:872] = jnp.zeros((8, LANES), F32)
+    if packed:
+        count = share // 64
+        low = lax.broadcasted_iota(jnp.int32, (14, LANES), 1) < 64
+        for k in range(32):
+            even = g2_ref[pl.ds(count * k, 14, stride=2), :]
+            odd = g2_ref[pl.ds(count * k + 1, 14, stride=2), :]
+            out_ref[k * 16:k * 16 + 14] = jnp.where(low, even, pltpu.roll(odd, 64, 1))
+    else:
+        out_ref[...] = g2_ref[...]
     for m in range(8):
         rows = slice(m * 128, m * 128 + 128)
         r0 = nn(lmat[128:384], d2_ref[m * 128:m * 128 + 256])
@@ -203,7 +224,8 @@
         g1_ref[dz] = acc
 
 
-def edge_kernel(share, packed, above_ref, lmat, d_ref, h_ref, g2_ref, g1_ref, grad_ref, out_ref, d2h, d1):
+def edge_kernel(packed, above_ref, lmat, d_ref, h_ref, g1_ref, grad_ref, *rest):
+    pay_ref, out_ref, d2h, d1, lines = rest if packed else (None,) + rest
     lane = lax.broadcasted_iota(jnp.int32, (64, LANES), 1)
     d2h[1024:1152] = jnp.zeros((128, LANES), BF)
     for y in range(8):
@@ -236,44 +258,47 @@
     if not packed:
         out_ref[...] = total
         return
-    count = share // 64
-    low = lax.broadcasted_iota(jnp.int32, (14, LANES), 1) < 64
+    lines[...] = pay_ref[...]
+    lines[pl.ds(14, 32, stride=16), :] = total
+    lines[pl.ds(15, 32, stride=16), :] = total - total.astype(BF).astype(F32)
+    out_ref[...] = lines[...].astype(BF).reshape(32, 16, LANES)
+
+
+def spread_kernel(count, full_ref, old_ref, kernel_ref, first_ref, lines):
+    columns = []
     for k in range(32):
-        even = g2_ref[pl.ds(count * k, 14, stride=2), :]
-        odd = g2_ref[pl.ds(count * k + 1, 14, stride=2), :]
-        out_ref[k, 0:14] = jnp.where(low, even, pltpu.roll(odd, 64, 1))
-        out_ref[k, 14:15] = total[k:k + 1]
-        out_ref[k, 15:16] = jnp.zeros((1, LANES), F32)
-
-
-def spread_kernel(count, full_ref, kernel_ref, first_ref, lines):
-    for k in range(32):
-        x = full_ref[k]
+        x = full_ref[k].astype(F32)
         lines[pl.ds(count * k, 14, stride=2), :] = x[0:14]
         lines[pl.ds(count * k + 1, 13, stride=2), :] = pltpu.roll(x, 64, 1)[0:13]
-    kernel_ref[...] = lines[0:864, 0:64]
-    columns = jnp.concatenate([full_ref[k, 14:15] for k in range(32)] + [jnp.zeros((96, LANES), F32)], axis=0)
-    turned = columns.T
+        columns.append(x[14:15] + x[15:16])
+    kernel_ref[...] = old_ref[...] - lines[0:864, 0:64]
+    turned = jnp.concatenate(columns + [jnp.zeros((96, LANES), F32)], axis=0).T
     for j in range(27):
         first_ref[j] = turned[j * 4:j * 4 + 4, 0:32]
 
 
 VMEM = pl.BlockSpec(memory_space=pltpu.VMEM)
-
-
-def call(kernel, outs, scratch, args):
+HBM = pl.BlockSpec(memory_space=pltpu.HBM)
+DMA = pltpu.SemaphoreType.DMA
+
+
+def call(kernel, outs, scratch, args, at=VMEM):
     return pl.pallas_call(
         kernel,
         out_shape=[pltpu.VMEM(s, t) if stays else jax.ShapeDtypeStruct(s, t) for s, t, stays in outs],
-        in_specs=[VMEM] * len(args),
+        in_specs=[at] * len(args),
         out_specs=[VMEM] * len(outs),
-        scratch_shapes=[pltpu.VMEM(s, t) for s, t in scratch],
+        scratch_shapes=[DMA(s) if t is DMA else pltpu.VMEM(s, t) for s, t in scratch],
         compiler_params=pltpu.CompilerParams(vmem_limit_bytes=40 * 1024 * 1024),
     )(*args)
 
 
 def stay(*arrays):
     return [pltpu.with_memory_space_constraint(a, pltpu.VMEM) for a in arrays]
+
+
+def stay_out(arrays):
+    return [pltpu.with_memory_space_constraint(a, pltpu.HBM) for a in arrays]
 
 
 def gather(values, count):
@@ -288,57 +313,60 @@
     below = along(volumes[0, :, -3:], "space", 1)
     deep = lambda n: ((n, 1056, LANES), BF, True)
     hidden = lambda n: ((n, 1632, LANES), BF, True)
-    sel, t1, w2t, lmat, d, h = call(
+    sel, t1, w2t, lmat, d, h, cot = call(
         own_kernel,
-        [((512, 512), BF, True), ((3, 128, 160), BF, True), ((3, 64, 288), BF, True), ((384, 256), BF, True), deep(8), hidden(3)],
-        [((4, 1056, LANES), F32), ((3, 40, 32), F32)],
-        (volumes[0], first_kernel.reshape(27, 4, 32), jnp.asarray(spread_taps(), BF), second_kernel.reshape(3, 288, 64)),
+        [((512, 512), BF, True), ((3, 128, 160), BF, True), ((3, 64, 288), BF, True), ((384, 256), BF, True), deep(8), hidden(3), ((64, 2, 8, LANES), BF, True)],
+        [((4, 1056, LANES), F32), ((3, 40, 32), F32), ((4, 8, 32, 512), BF), ((27, 4, 32), BF), ((36, 1024), BF), ((3, 288, 64), F32), ((6,), DMA)],
+        stay_out((volumes[0], first_kernel.reshape(27, 4, 32), jnp.asarray(spread_taps(), BF), second_kernel.reshape(3, 288, 64), cotangent[0])), HBM,
     )
-    sel, t1, w2t, lmat, d, h = stay(sel, t1, w2t, lmat, d, h)
+    sel, t1, w2t, lmat, d, h, cot = stay(sel, t1, w2t, lmat, d, h, cot)
     dl, hl, d2, edge, a0 = call(
         halo_kernel,
         [deep(3), hidden(2), ((1152, LANES), BF, True), ((512, LANES), BF, False), ((64, 8, LANES), BF, True)],
         [((3, 1056, LANES), F32), ((512, LANES), F32), ((512, LANES), F32)],
-        (below, cotangent[0], sel, t1, w2t, d, h),
+        (below, cot, sel, t1, w2t, d, h),
     )
     above = along(edge, "space", -1)
     dl, hl, d2, a0 = stay(dl, hl, d2, a0)
     act, g2, g1, grad = call(
-        inner_kernel,
-        [((64, 2, 8, LANES), BF, False), ((872, LANES), F32, packed), ((3, 128, 160), F32, True), ((1024, LANES), F32, True)],
-        [((1152, LANES), BF), ((3, 1024, LANES), BF), ((512, LANES), F32), ((512, LANES), F32)],
-        (cotangent[0], w2t, lmat, d, h, dl, hl, d2, a0),
+        functools.partial(inner_kernel, share, packed),
+        [((64, 2, 8, LANES), BF, False), ((512, LANES) if packed else (872, LANES), F32, packed), ((3, 128, 160), F32, True), ((1024, LANES), F32, True)],
+        [((872, LANES), F32), ((1152, LANES), BF), ((3, 1024, LANES), BF), ((512, LANES), F32), ((512, LANES), F32)],
+        (cot, w2t, lmat, d, h, dl, hl, d2, a0),
     )
     g1, grad = stay(g1, grad)
     if packed:
         (g2,) = stay(g2)
     (out,) = call(
-        functools.partial(edge_kernel, share, packed),
-        [((32, 16, LANES) if packed else (32, LANES), F32, False)],
-        [((1152, LANES), BF), ((1024, LANES), BF)],
-        (above, lmat, d, h, g2, g1, grad),
+        functools.partial(edge_kernel, packed),
+        [((32, 16, LANES), BF, False) if packed else ((32, LANES), F32, False)],
+        [((1152, LANES), BF), ((1024, LANES), BF), ((512, LANES), F32)],
+        (above, lmat, d, h, g1, grad) + ((g2,) if packed else ()),
     )
     if packed:
-        both = lax.all_to_all(out, AXES, 0, 0, tiled=True).sum(0).reshape(-1)
+        both = lax.all_to_all(out, AXES, 0, 0, tiled=True).astype(F32).sum(0)
+        one = both[14] + both[15]
+        both = both.reshape(-1)
     else:
         one = out[:, :108].T.reshape(-1)
         one = jnp.pad(one, (0, -one.shape[0] % count)).reshape(count, -1)
         both = jnp.concatenate([g2[:864, :64].reshape(count, share), one], axis=1)
         both = lax.all_to_all(both, AXES, 0, 0, tiled=True).sum(0)
     grad_share = both[:share]
-    offset = lax.axis_index(AXES) * share
     new_first = BETA_FIRST * first_moment + (1.0 - BETA_FIRST) * grad_share
     new_second = BETA_SECOND * second_moment + (1.0 - BETA_SECOND) * grad_share * grad_share
-    kernel_share = lax.dynamic_slice_in_dim(second_kernel.reshape(-1), offset, share, 0)
-    updated = kernel_share - LEARN_RATE * new_first / (jnp.sqrt(new_second) + EPSILON)
-    send = jnp.concatenate([updated, both[share:]])
+    change = LEARN_RATE * new_first / (jnp.sqrt(new_second) + EPSILON)
     if packed:
-        full = gather(send.reshape(16, LANES), count)
+        tail = jnp.stack([one, one - lax.reduce_precision(one, 8, 7)])
+        send = jnp.concatenate([jnp.pad(change, (0, 64)).reshape(14, LANES), tail]).astype(BF)
+        full = gather(send, count)
         new_kernel, first_gradient = call(
             functools.partial(spread_kernel, share // 64),
-            [((864, 64), F32, False), ((27, 4, 32), F32, False)], [((880, LANES), F32)], (full,))
+            [((864, 64), F32, False), ((27, 4, 32), F32, False)], [((880, LANES), F32)], (full, second_kernel.reshape(864, 64)))
     else:
-        full = gather(send, count)
+        offset = lax.axis_index(AXES) * share
+        kernel_share = lax.dynamic_slice_in_dim(second_kernel.reshape(-1), offset, share, 0)
+        full = gather(jnp.concatenate([kernel_share - change, both[share:]]), count)
         new_kernel = full[:, :share]
         first_gradient = full[:, share:].reshape(-1)[:first_kernel.size]
     return (act[None], first_gradient.reshape(first_kernel.shape), new_kernel.reshape(second_kernel.shape), new_first, new_second)

time: 55.8 us -> 47.2 us (0.85)
  blocking collectives: 12.7 us -> 27.3 us
  waiting for transfers between devices: 10.3 us -> 0.01 us
  starting transfers between devices: 12.8 us -> 3.67 us
  local copies, waits for them, and re-layouts: 5.16 us -> 1.07 us
    all_to_all x0 -> x1, blocking collectives: none -> 17.4 us  [shards(): both = lax.all_to_all(out, AXES, 0, 0, tiled=True).astype(F32).sum(0)]
    all_to_all x1 -> x0, waiting for transfers between devices: 10.2 us -> none  [shards(): both = lax.all_to_all(out, AXES, 0, 0, tiled=True).sum(0).reshape(-1)]
    all_to_all x1 -> x0, starting transfers between devices: 9.12 us -> none  [shards(): both = lax.all_to_all(out, AXES, 0, 0, tiled=True).sum(0).reshape(-1)]
    unnamed x16 -> x6, local copies, waits for them, and re-layouts: 3.88 us -> 0.01 us
    all_to_all x1, blocking collectives: 12.7 us -> 9.88 us  [gather(): return lax.all_to_all(wide, AXES, 0, 0, tiled=True)]
    another operation x0 -> x2, other arithmetic: none -> 0.62 us
    sub x1 -> x0, other arithmetic: 0.61 us -> none  [shards(): kernel_share - LEARN_RATE * new_first / (jnp.sqrt(new_second) + EPSILON)]
  transfers between devices with their start and end apart: 3 -> 2, of which waited for: 2 -> 0; matrix products, arithmetic and copies ran while one was open for 0% -> 0% of each run, Pallas kernels for 15% -> 20%
where the time goes in v3:
time: 47.2 us; the launch traced here: 46.9 us
  blocking collectives  27.3 us (58%)
  Pallas kernels  13.5 us (29%)
  starting transfers between devices  3.67 us (8%)
  local copies, waits for them, and re-layouts  1.07 us (2%)
  between operations  0.71 us (2%)
  other arithmetic  0.67 us (1%)
    all_to_all x1, blocking collectives, shards(): both = lax.all_to_all(out, AXES, 0, 0, tiled=True).astype(F32).sum(0)  17.4 us
    pallas_call x5, Pallas kernels, call(): pl.pallas_call(kernel, out_shape=[pltpu.VMEM(s, t) if stays else jax.Shap...  13.5 us
    all_to_all x1, blocking collectives, gather(): return lax.all_to_all(wide, AXES, 0, 0, tiled=True)  9.88 us
    ppermute x2, starting transfers between devices, along(): lax.ppermute(value, axis, [(source, source + steps) for source in range(f...  3.67 us
    squeeze x1, local copies, waits for them, and re-layouts, shards(): below = along(volumes[0, :, -3:], 'space', 1)  1.03 us
  transfers between devices with their start and end apart: 2, of which 0 were waited for; matrix products, arithmetic and copies ran while one was open for 0% of the time, Pallas kernels for 20%

profile of v3, /device:TPU:0, one launch (start us, length us, event | category | flops | bytes accessed | tf_op | source)
XLA Modules:
  0.0 46.9 jit_solution(14333969584840697004)
XLA Ops:
  0.6 1.0 %slice_bitcast_fusion = bf16[4,3,32,512]{3,2,1,0:T(8,128)(2,1)S(1)} fusion(bf16[1,4,8,32,512]{4,3,2,1,0:T(8,128)(2,1)} %param.7), kind=kLoop, calls=%fused_computation | loop fusion | bytes 786432 | tf_op jit(solution)/shard_map/squeeze | solution.py:313
  1.7 2.4 %collective-permute-start = (bf16[4,3,32,512]{3,2,1,0:T(8,128)(2,1)S(1)}, bf16[4,3,32,512]{3,2,1,0:T(8,128)(2,1)S(1)}, u32[]{:S(2)}, u32[]{:S(2)}) collective-permute-start(bf16[4,3,32,512]{3,2,1,0:T(8,128)(2,1)S(1)} %slice_bitcast_fusion), channel_id=1, source_target_pairs={{0,1},{1,2},{2,3},{3,4},{4,5},{5,6},{6,7},{8,9},{9,10},{10,11},{11... | collective-permute-start | bytes 1179656 | tf_op jit(solution)/shard_map/ppermute | solution.py:24
  4.1 5.3 %shard_map.110 = (bf16[512,512]{1,0:T(8,128)(2,1)S(1)}, bf16[3,128,160]{2,1,0:T(8,128)(2,1)S(1)}, bf16[3,64,288]{2,1,0:T(8,128)(2,1)S(1)}, bf16[384,256]{1,0:T(8...) custom-call(bf16[4,8,32,512]{3,2,1,0:T(8,128)(2,1)} %bitcast.15, ...), custom_call_target="tpu_custom_call" | custom-call | tf_op jit(solution)/shard_map/pallas_call | solution.py:286
  9.3 0.0 collective-permute-done.vh_ref
  9.3 2.1 %shard_map.111 = (bf16[3,1056,128]{2,1,0:T(8,128)(2,1)S(1)}, bf16[2,1632,128]{2,1,0:T(8,128)(2,1)S(1)}, bf16[1152,128]{1,0:T(8,128)(2,1)S(1)}, bf16[512,128]{1,0:T(8,128)(2,1)S(1)}, bf16[64,8,128]{2,1,0:T(8,128)(2,1)S(1)}) custom-call(bf16[4,3,32,512]{3,2,1,0:T(8,128)(2,1)S(1)} %collective-permute-done.vh_ref, ...), custom_call_target="tpu_custom_call" | custom-call | tf_op jit(solution)/shard_map/pallas_call | solution.py:286
  11.4 1.3 %collective-permute-start.1 = (bf16[512,128]{1,0:T(8,128)(2,1)S(1)}, bf16[512,128]{1,0:T(8,128)(2,1)S(1)}, u32[]{:S(2)}, u32[]{:S(2)}) collective-permute-start(bf16[512,128]{1,0:T(8,128)(2,1)S(1)} %get-tuple-element.35), channel_id=1, source_target_pairs={{1,0},{2,1},{3,2},{4,3},{5,4},{6,5},{7,6},{9,8},{10,9},{11,10},{12... | collective-permute-start | bytes 393224 | tf_op jit(solution)/shard_map/ppermute | solution.py:24
  12.7 4.1 %shard_map.112 = (bf16[64,2,8,128]{3,2,1,0:T(8,128)(2,1)}, f32[512,128]{1,0:T(8,128)S(1)}, f32[3,128,160]{2,1,0:T(8,128)S(1)}, f32[1024,128]{1,0:T(8,128)S(1)}) custom-call(bf16[64,2,8,128]{3,2,1,0:T(8,128)(2,1)S(1)} %get-tuple-element.23.cot_ref, bf16[3,64,288]{2,1,0:T(8,128)(2,1)S(1)} %get-tuple-element.24.w2t, ...), custom_call_target="tpu_custom_call" | custom-call | tf_op jit(solution)/shard_map/pallas_call | solution.py:286
  16.8 0.0 collective-permute-done.1.above_ref
  16.8 0.0 copy-start.1
  16.8 0.0 copy-start.2
  16.8 0.0 copy-start
  16.8 1.1 %shard_map.113 = bf16[32,16,128]{2,1,0:T(8,128)(2,1)S(1)} custom-call(bf16[512,128]{1,0:T(8,128)(2,1)S(1)} %collective-permute-done.1.above_ref, bf16[384,256]{1,0:T(8,128)(2,1)S(1)} %get-tuple-element.25.lmat, bf16[8,1056,128]{2,1,0:T(8,128)(2,1)S(1)} %get-tuple-element.26.d_ref, bf16[3,1632,128]{2,1,0:T(8,128)(2,1)S(1)} %get-tuple-element.27.h_ref, ...), custom_call_target="tpu_custom_call" | custom-call | tf_op jit(solution)/shard_map/pallas_call | solution.py:286
  18.0 17.4 %all_to_all.10 = bf16[32,16,128]{2,1,0:T(8,128)(2,1)S(1)} all-to-all(bf16[32,16,128]{2,1,0:T(8,128)(2,1)S(1)} %shard_map.113), channel_id=1, replica_groups=mesh['dp'=4,'space'=8] {'dp','space'}, dimensions={0} | all-to-all | bytes 262144 | tf_op jit(solution)/shard_map/all_to_all | solution.py:347
  35.4 0.0 copy-done.1
  35.5 0.0 copy-done.2
  35.5 0.6 %divide_convert_fusion = (bf16[1728]{0:T(1024)(128)(2,1)S(1)}, f32[1728]{0:T(1024)}, f32[1728]{0:T(1024)}) fusion(f32[2048]{0:T(1024)S(1)} %bitcast.17, f32[1728]{0:T(1024)S(1)} %copy-done.1, f32[1728]{0:T(1024)S(1)} %copy-done.2), kind=kLoop, calls=%fused_computation.4 | loop fusion | flops 19008 | bytes 38016 | tf_op jit(solution)/shard_map/convert.4
  36.1 9.9 %all_to_all.11.full_ref = bf16[32,16,128]{2,1,0:T(8,128)(2,1)S(1)} all-to-all(bf16[32,16,128]{2,1,0:T(8,128)(2,1)S(1)} %broadcast_in_dim.10), channel_id=1, replica_groups=mesh['dp'=4,'space'=8] {'dp','space'}, dimensions={0} | all-to-all | bytes 262144 | tf_op jit(solution)/shard_map/all_to_all | solution.py:306
  46.0 0.0 copy-done
  46.0 0.9 %shard_map.114 = (f32[864,64]{1,0:T(8,128)}, f32[27,4,32]{2,1,0:T(4,128)}) custom-call(bf16[32,16,128]{2,1,0:T(8,128)(2,1)S(1)} %all_to_all.11.full_ref, f32[864,64]{1,0:T(8,128)S(1)} %bitcast.14), custom_call_target="tpu_custom_call" | custom-call | tf_op jit(solution)/shard_map/pallas_call | solution.py:286
  (5 shorter events, 0.1 us)
Async XLA Ops:
  1.7 7.7 %collective-permute-start = (bf16[4,3,32,512]{3,2,1,0:T(8,128)(2,1)S(1)}, bf16[4,3,32,512]{3,2,1,0:T(8,128)(2,1)S(1)}, u32[]{:S(2)}, u32[]{:S(2)}) collective-permute-start(bf16[4,3,32,512]{3,2,1,0:T(8,128)(2,1)S(1)} %slice_bitcast_fusion), channel_id=1, source_target_pairs={{0,1},{1,2},{2,3},{3,4},{4,5},{5,6},{6,7},{8,9},{9,10},{10,11},{11... | collective-permute-start | bytes 1179656 | tf_op jit(solution)/shard_map/ppermute | solution.py:24
  11.4 5.4 %collective-permute-start.1 = (bf16[512,128]{1,0:T(8,128)(2,1)S(1)}, bf16[512,128]{1,0:T(8,128)(2,1)S(1)}, u32[]{:S(2)}, u32[]{:S(2)}) collective-permute-start(bf16[512,128]{1,0:T(8,128)(2,1)S(1)} %get-tuple-element.35), channel_id=1, source_target_pairs={{1,0},{2,1},{3,2},{4,3},{5,4},{6,5},{7,6},{9,8},{10,9},{11,10},{12... | collective-permute-start | bytes 393224 | tf_op jit(solution)/shard_map/ppermute | solution.py:24
  16.8 18.6 %copy-start.1 = (f32[1728]{0:T(1024)S(1)}, f32[1728]{0:T(1024)}, u32[]{:S(2)}) copy-start(f32[1728]{0:T(1024)} %param.11) | copy-start | bytes 20740
  16.8 18.6 %copy-start.2 = (f32[1728]{0:T(1024)S(1)}, f32[1728]{0:T(1024)}, u32[]{:S(2)}) copy-start(f32[1728]{0:T(1024)} %param.12) | copy-start | bytes 20740
  16.8 29.2 %copy-start = (f32[3,3,3,32,64]{4,3,2,1,0:T(8,128)S(1)}, f32[3,3,3,32,64]{4,3,2,1,0:T(8,128)}, u32[]{:S(2)}) copy-start(f32[3,3,3,32,64]{4,3,2,1,0:T(8,128)} %param.9) | copy-start | bytes 663556

commit v4 on v3

--- a/solution.py
+++ b/solution.py
@@ -16,6 +16,9 @@
 F32 = jnp.float32
 AXES = ("dp", "space")
 LANES = 128
+SLOTS = 20
+REACH = 112
+DEEP = 672
 
 
 def along(value, axis, steps):
@@ -41,14 +44,14 @@
 
 
 def spread_taps():
-    table = np.zeros((3, 3, 4, 2, 2, 256), np.float32)
+    table = np.zeros((3, 3, 4, 2, 2, LANES), np.float32)
     for dy in range(3):
         for dx in range(3):
             for c in range(4):
                 for row in range(2):
                     for p in range(2):
-                        table[dy, dx, c, row, p, (2 * row + dy) * 32 + (2 * p + dx) * 4 + c] = 1
-    return table.reshape(36, 1024)
+                        table[dy, dx, c, row, p, (2 * row + dy) * SLOTS + (2 * p + dx) * 4 + c] = 1
+    return table.reshape(36, 512)
 
 
 def repack(source, first, count, sel, stage, out, to):
@@ -59,12 +62,18 @@
         for i in range(count):
             for c in range(4):
                 block = part[i * 128 + c * 32:i * 128 + c * 32 + 32]
-                stage[i, pl.ds(32 + (r + 1) * 4 + c, 32, stride=32), :] = block
+                stage[i, pl.ds(SLOTS + (r + 1) * 4 + c, 32, stride=SLOTS), :] = block
                 if r == 3:
                     moved = jnp.where(lane == 0, 0.0, pltpu.roll(block, 1, 1))
-                    stage[i, pl.ds(32 + c, 32, stride=32), :] = moved
+                    stage[i, pl.ds(SLOTS + c, 32, stride=SLOTS), :] = moved
     for i in range(count):
         out[to + i] = stage[i].astype(BF)
+
+
+def clear(stage):
+    for i in range(stage.shape[0]):
+        stage[i, 0:24] = jnp.zeros((24, LANES), F32)
+        stage[i, 656:DEEP] = jnp.zeros((DEEP - 656, LANES), F32)
 
 
 def first_section(t1, planes, outs):
@@ -90,7 +99,7 @@
 
 
 def pair_rows(*places):
-    return lambda m: beside(*[ref[z, m * 128:m * 128 + 160] for ref, z in places])
+    return lambda m: beside(*[ref[z, m * 4 * SLOTS:m * 4 * SLOTS + REACH] for ref, z in places])
 
 
 def second_section(w2t, planes, cot_ref, z, rows_c, rows_a, put):
@@ -106,8 +115,8 @@
         put(y, delta.astype(BF), left.astype(BF))
 
 
-def own_kernel(v_hbm, w1_hbm, e_hbm, w2_hbm, cot_hbm, sel, t1, w2t, lmat, d_ref, h_ref, cot_ref,
-               stage, w1s, v_ref, w1_ref, e_ref, w2_ref, sems):
+def own_kernel(v_hbm, w1_hbm, e_hbm, w2_hbm, cot_hbm, sel, t1, w2t, lmat, d_ref, h_ref, cot_ref, d2_ref, edge_ref, act_ref,
+               stage, rows_c, rows_a, w1s, v_ref, w1_ref, e_ref, w2_ref, sems):
     moves = [pltpu.make_async_copy(source, target, sems.at[i]) for i, (source, target) in enumerate((
         (w1_hbm, w1_ref), (e_hbm, e_ref), (w2_hbm, w2_ref),
         (v_hbm.at[:, 0:4], v_ref.at[:, 0:4]), (v_hbm.at[:, 4:8], v_ref.at[:, 4:8]), (cot_hbm, cot_ref)))]
@@ -118,7 +127,7 @@
     base = row - 4 * lane
     for r in range(4):
         sel[:, r * LANES:(r + 1) * LANES] = jnp.where(base == r, 1.0, 0.0).astype(BF)
-    stage[...] = jnp.zeros_like(stage)
+    clear(stage)
     moves[0].wait()
     moves[1].wait()
     for j in range(27):
@@ -126,7 +135,7 @@
     for dz in range(3):
         taps = tn(w1s[dz, 0:36].astype(BF), e_ref[...]).astype(BF)
         for b in range(4):
-            t1[dz, b * 32:(b + 1) * 32, :] = taps[:, b * 256:b * 256 + 160]
+            t1[dz, b * 32:(b + 1) * 32, :] = taps[:, b * LANES:b * LANES + REACH]
     eye = jnp.where(lax.broadcasted_iota(jnp.int32, (64, 64), 0) == lax.broadcasted_iota(jnp.int32, (64, 64), 1), 1.0, 0.0).astype(BF)
     step = lax.broadcasted_iota(jnp.int32, (64, LANES), 1) - lax.broadcasted_iota(jnp.int32, (64, LANES), 0)
     to_low = jnp.where(step == 0, 1.0, 0.0).astype(BF)
@@ -152,10 +161,25 @@
     first_section(t1, [pair_rows((d_ref, 1 + dz), (d_ref, 3 + dz)) for dz in range(3)], [(h_ref, 0), (h_ref, 1)])
     first_section(t1, [pair_rows((d_ref, 5 + dz)) for dz in range(3)], [(h_ref, 2)])
     moves[5].wait()
-
-
-def halo_kernel(vh_ref, cot_ref, sel, t1, w2t, d_ref, h_ref, dl_ref, hl_ref, d2_ref, edge_ref, a0_ref, stage, rows_c, rows_a):
-    stage[...] = jnp.zeros_like(stage)
+    d2_ref[1024:1152] = jnp.zeros((128, LANES), BF)
+
+    def put(y, delta, left):
+        d2_ref[y * 128:y * 128 + 64] = delta
+        d2_ref[y * 128 + 64:y * 128 + 128] = left
+        edge_ref[y * 64:y * 64 + 64] = delta
+
+    second_section(w2t, [(h_ref, 0), (h_ref, 1), (h_ref, 2)], cot_ref, 1, rows_c, rows_a, put)
+    act_ref[...] = rows_a[...].astype(BF).reshape(64, 8, LANES)
+
+
+def slopes(ref, z, m):
+    parts = [jnp.where(ref[z, (2 * m + i + 1) * 96 + 32:(2 * m + i + 1) * 96 + 96].astype(F32) > 0, 1.0, SLOPE) for i in range(2)]
+    return jnp.concatenate(parts, axis=0)
+
+
+def inner_kernel(share, packed, vh_ref, cot_ref, sel, t1, w2t, lmat, d_ref, h_ref, d2n, upper_ref,
+                 act_ref, out_ref, g1_ref, grad_ref, dl_ref, hl_ref, stage, g2_ref, d2_ref, d1, rows_c, rows_a):
+    clear(stage)
     repack(vh_ref, 0, 3, sel, stage, dl_ref, 0)
     first_section(t1, [pair_rows((dl_ref, 0), (dl_ref, 2)), pair_rows((dl_ref, 1), (d_ref, 0)), pair_rows((dl_ref, 2), (d_ref, 1))],
                   [(hl_ref, 0), (hl_ref, 1)])
@@ -164,37 +188,19 @@
     def put(y, delta, left):
         d2_ref[y * 128:y * 128 + 64] = delta
         d2_ref[y * 128 + 64:y * 128 + 128] = left
-        edge_ref[y * 64:y * 64 + 64] = delta
 
     second_section(w2t, [(hl_ref, 0), (hl_ref, 1), (h_ref, 0)], cot_ref, 0, rows_c, rows_a, put)
-    a0_ref[...] = rows_a[...].astype(BF).reshape(64, 8, LANES)
-
-
-def slopes(ref, z, m):
-    parts = [jnp.where(ref[z, (2 * m + i + 1) * 96 + 32:(2 * m + i + 1) * 96 + 96].astype(F32) > 0, 1.0, SLOPE) for i in range(2)]
-    return jnp.concatenate(parts, axis=0)
-
-
-def inner_kernel(share, packed, cot_ref, w2t, lmat, d_ref, h_ref, dl_ref, hl_ref, d2_ref, a0_ref,
-                 act_ref, out_ref, g1_ref, grad_ref, g2_ref, d2n, d1, rows_c, rows_a):
-    d2n[1024:1152] = jnp.zeros((128, LANES), BF)
-
-    def put(y, delta, left):
-        d2n[y * 128:y * 128 + 64] = delta
-        d2n[y * 128 + 64:y * 128 + 128] = left
-
-    second_section(w2t, [(h_ref, 0), (h_ref, 1), (h_ref, 2)], cot_ref, 1, rows_c, rows_a, put)
-    act_ref[:, 0] = a0_ref[...]
-    act_ref[:, 1] = rows_a[...].astype(BF).reshape(64, 8, LANES)
+    act_ref[:, 0] = rows_a[...].astype(BF).reshape(64, 8, LANES)
+    act_ref[:, 1] = upper_ref[...]
     lower = [(hl_ref, 0), (hl_ref, 1), (h_ref, 0)]
     for dz in range(3):
-        acc = jnp.zeros((288, LANES), F32)
+        acc = jnp.zeros((288, 64), F32)
         ref, z = lower[dz]
         for y in range(8):
             a = beside(ref[z, y * 192:y * 192 + 288], h_ref[dz, y * 192:y * 192 + 288])
-            b = beside(d2_ref[y * 128:y * 128 + 128], d2n[y * 128:y * 128 + 128])
+            b = beside(d2_ref[y * 128:y * 128 + 64], d2n[y * 128:y * 128 + 64])
             acc += nt(a, b)
-        g2_ref[dz * 288:dz * 288 + 288] = acc
+        g2_ref[dz * 288:dz * 288 + 288, 0:64] = acc
     g2_ref[864:872] = jnp.zeros((8, LANES), F32)
     if packed:
         count = share // 64
@@ -207,15 +213,15 @@
         out_ref[...] = g2_ref[...]
     for m in range(8):
         rows = slice(m * 128, m * 128 + 128)
-        r0 = nn(lmat[128:384], d2_ref[m * 128:m * 128 + 256])
-        r1 = nn(lmat[...], d2n[m * 128:m * 128 + 256])
-        d1[0, rows] = (r0[0:128] * slopes(hl_ref, 1, m)).astype(BF)
-        d1[1, rows] = ((r0[128:256] + r1[0:128]) * slopes(h_ref, 0, m)).astype(BF)
+        r = nn(lmat[...], beside(d2_ref[m * 128:m * 128 + 256], d2n[m * 128:m * 128 + 256]))
+        r0, r1 = r[:, 0:LANES], r[:, LANES:2 * LANES]
+        grad_ref[rows] = r0[0:128]
+        d1[0, rows] = (r0[128:256] * slopes(hl_ref, 1, m)).astype(BF)
+        d1[1, rows] = ((r0[256:384] + r1[0:128]) * slopes(h_ref, 0, m)).astype(BF)
         d1[2, rows] = (r1[128:256] * slopes(h_ref, 1, m)).astype(BF)
-        grad_ref[rows] = r1[256:384]
     lower = [(dl_ref, 2), (d_ref, 0), (d_ref, 1)]
     for dz in range(3):
-        acc = jnp.zeros((128, 160), F32)
+        acc = jnp.zeros((128, REACH), F32)
         two, one = pair_rows(lower[dz], (d_ref, 1 + dz)), pair_rows((d_ref, 3 + dz))
         for m in range(8):
             rows = slice(m * 128, m * 128 + 128)
@@ -223,36 +229,47 @@
             acc += nt(d1[2, rows], one(m))
         g1_ref[dz] = acc
 
-
-def edge_kernel(packed, above_ref, lmat, d_ref, h_ref, g1_ref, grad_ref, *rest):
+    @pl.when(lax.axis_index("space") == lax.axis_size("space") - 1)
+    def _():
+        for m in range(8):
+            rows = slice(m * 128, m * 128 + 128)
+            d1[0, rows] = (nn(lmat[256:384], d2n[m * 128:m * 128 + 256]) * slopes(h_ref, 2, m)).astype(BF)
+        for dz in range(3):
+            acc = g1_ref[dz]
+            one = pair_rows((d_ref, 5 + dz))
+            for m in range(8):
+                acc += nt(d1[0, m * 128:m * 128 + 128], one(m))
+            g1_ref[dz] = acc
+
+
+def edge_kernel(packed, under_ref, lmat, dl_ref, hl_ref, g1_ref, grad_ref, *rest):
     pay_ref, out_ref, d2h, d1, lines = rest if packed else (None,) + rest
     lane = lax.broadcasted_iota(jnp.int32, (64, LANES), 1)
     d2h[1024:1152] = jnp.zeros((128, LANES), BF)
     for y in range(8):
-        low = above_ref[y * 64:y * 64 + 64]
+        low = under_ref[y * 64:y * 64 + 64]
         left = jnp.where(lane == LANES - 1, 0.0, pltpu.roll(low.astype(F32), LANES - 1, 1))
         d2h[y * 128:y * 128 + 64] = low
         d2h[y * 128 + 64:y * 128 + 128] = left.astype(BF)
     for m in range(8):
         rows = slice(m * 128, m * 128 + 128)
-        grad = grad_ref[rows] + nn(lmat[0:128], d2h[m * 128:m * 128 + 256])
-        d1[rows] = (grad * slopes(h_ref, 2, m)).astype(BF)
+        grad = grad_ref[rows] + nn(lmat[256:384], d2h[m * 128:m * 128 + 256])
+        d1[rows] = (grad * slopes(hl_ref, 0, m)).astype(BF)
     lane = lax.broadcasted_iota(jnp.int32, (32, LANES), 1)
     total = jnp.zeros((32, LANES), F32)
     for dz in range(3):
         acc = g1_ref[dz]
-        rows_of = pair_rows((d_ref, 5 + dz))
+        rows_of = pair_rows((dl_ref, dz))
         for m in range(8):
             acc += nt(d1[m * 128:m * 128 + 128], rows_of(m))
-        wide = (acc[:, 0:128], jnp.concatenate([acc[:, 128:160], jnp.zeros((128, 96), F32)], axis=1))
+        wide = jnp.concatenate([acc, jnp.zeros((128, LANES - REACH), F32)], axis=1)
         for dy in range(3):
             to = (dz * 3 + dy) * 12
             part = jnp.zeros((32, LANES), F32)
             for i in range(2):
                 for p in range(2):
-                    y = 2 * i + dy
-                    block = wide[y // 4][(2 * i + p) * 32:(2 * i + p) * 32 + 32]
-                    shift = (to - ((y % 4) * 32 + 8 * p)) % LANES
+                    block = wide[(2 * i + p) * 32:(2 * i + p) * 32 + 32]
+                    shift = (to - ((2 * i + dy) * SLOTS + 8 * p)) % LANES
                     part += block if shift == 0 else pltpu.roll(block, shift, 1)
             total = jnp.where((lane >= to) & (lane < to + 12), part, total)
     if not packed:
@@ -289,7 +306,7 @@
         in_specs=[at] * len(args),
         out_specs=[VMEM] * len(outs),
         scratch_shapes=[DMA(s) if t is DMA else pltpu.VMEM(s, t) for s, t in scratch],
-        compiler_params=pltpu.CompilerParams(vmem_limit_bytes=40 * 1024 * 1024),
+        compiler_params=pltpu.CompilerParams(vmem_limit_bytes=32 * 1024 * 1024),
     )(*args)
 
 
@@ -311,37 +328,33 @@
     share = first_moment.shape[0]
     packed = count == 32 and share == 1728
     below = along(volumes[0, :, -3:], "space", 1)
-    deep = lambda n: ((n, 1056, LANES), BF, True)
+    deep = lambda n: ((n, DEEP, LANES), BF, True)
     hidden = lambda n: ((n, 1632, LANES), BF, True)
-    sel, t1, w2t, lmat, d, h, cot = call(
+    plane = ((64, 8, LANES), BF, True)
+    spread = ((1152, LANES), BF)
+    flat = ((512, LANES), F32)
+    sel, t1, w2t, lmat, d, h, cot, d2, edge, upper = call(
         own_kernel,
-        [((512, 512), BF, True), ((3, 128, 160), BF, True), ((3, 64, 288), BF, True), ((384, 256), BF, True), deep(8), hidden(3), ((64, 2, 8, LANES), BF, True)],
-        [((4, 1056, LANES), F32), ((3, 40, 32), F32), ((4, 8, 32, 512), BF), ((27, 4, 32), BF), ((36, 1024), BF), ((3, 288, 64), F32), ((6,), DMA)],
+        [((512, 512), BF, True), ((3, 128, REACH), BF, True), ((3, 64, 288), BF, True), ((384, 256), BF, True), deep(8), hidden(3),
+         ((64, 2, 8, LANES), BF, True), spread + (True,), ((512, LANES), BF, False), plane],
+        [((4, DEEP, LANES), F32), flat, flat, ((3, 40, 32), F32),
+         ((4, 8, 32, 512), BF), ((27, 4, 32), BF), ((36, 512), BF), ((3, 288, 64), F32), ((6,), DMA)],
         stay_out((volumes[0], first_kernel.reshape(27, 4, 32), jnp.asarray(spread_taps(), BF), second_kernel.reshape(3, 288, 64), cotangent[0])), HBM,
     )
-    sel, t1, w2t, lmat, d, h, cot = stay(sel, t1, w2t, lmat, d, h, cot)
-    dl, hl, d2, edge, a0 = call(
-        halo_kernel,
-        [deep(3), hidden(2), ((1152, LANES), BF, True), ((512, LANES), BF, False), ((64, 8, LANES), BF, True)],
-        [((3, 1056, LANES), F32), ((512, LANES), F32), ((512, LANES), F32)],
-        (below, cot, sel, t1, w2t, d, h),
+    cot, sel, t1, w2t, lmat, d, h, d2, upper = stay(cot, sel, t1, w2t, lmat, d, h, d2, upper)
+    under = along(edge, "space", 1)
+    act, g2, g1, grad, dl, hl = call(
+        functools.partial(inner_kernel, share, packed),
+        [((64, 2, 8, LANES), BF, False), ((512, LANES) if packed else (872, LANES), F32, packed), ((3, 128, REACH), F32, True),
+         ((1024, LANES), F32, True), deep(3), hidden(2)],
+        [((3, DEEP, LANES), F32), ((872, LANES), F32), spread, ((3, 1024, LANES), BF), flat, flat],
+        [below, cot, sel, t1, w2t, lmat, d, h, d2, upper],
     )
-    above = along(edge, "space", -1)
-    dl, hl, d2, a0 = stay(dl, hl, d2, a0)
-    act, g2, g1, grad = call(
-        functools.partial(inner_kernel, share, packed),
-        [((64, 2, 8, LANES), BF, False), ((512, LANES) if packed else (872, LANES), F32, packed), ((3, 128, 160), F32, True), ((1024, LANES), F32, True)],
-        [((872, LANES), F32), ((1152, LANES), BF), ((3, 1024, LANES), BF), ((512, LANES), F32), ((512, LANES), F32)],
-        (cot, w2t, lmat, d, h, dl, hl, d2, a0),
-    )
-    g1, grad = stay(g1, grad)
-    if packed:
-        (g2,) = stay(g2)
     (out,) = call(
         functools.partial(edge_kernel, packed),
         [((32, 16, LANES), BF, False) if packed else ((32, LANES), F32, False)],
-        [((1152, LANES), BF), ((1024, LANES), BF), ((512, LANES), F32)],
-        (above, lmat, d, h, g1, grad) + ((g2,) if packed else ()),
+        [spread, ((1024, LANES), BF), flat],
+        [under, lmat] + stay(dl, hl, g1, grad) + (stay(g2) if packed else []),
     )
     if packed:
         both = lax.all_to_all(out, AXES, 0, 0, tiled=True).astype(F32).sum(0)

time: 47.2 us -> 43.4 us (0.919)
  blocking collectives: 27.3 us -> 22.9 us
  starting transfers between devices: 3.67 us -> 6.96 us
  Pallas kernels: 13.5 us -> 10.9 us
    all_to_all x1, blocking collectives: 17.4 us -> 13 us  [shards(): both = lax.all_to_all(out, AXES, 0, 0, tiled=True).astype(F32).sum(0)]
    ppermute x2, starting transfers between devices: 3.67 us -> 6.96 us  [along(): lax.ppermute(value, axis, [(source, source + steps) for source in range(f...]
    pallas_call x5 -> x4, Pallas kernels: 13.5 us -> 10.9 us  [call(): pl.pallas_call(kernel, out_shape=[pltpu.VMEM(s, t) if stays else jax.Shap...]
  transfers between devices with their start and end apart: 2 -> 2, of which waited for: 0 -> 0; matrix products, arithmetic and copies ran while one was open for 0% -> 0% of each run, Pallas kernels for 20% -> 21%
where the time goes in v4:
time: 43.4 us; the launch traced here: 43.2 us
  blocking collectives  22.9 us (53%)
  Pallas kernels  10.9 us (25%)
  starting transfers between devices  6.96 us (16%)
  local copies, waits for them, and re-layouts  1.07 us (2%)
  between operations  0.72 us (2%)
  other arithmetic  0.67 us (2%)
    all_to_all x1, blocking collectives, shards(): both = lax.all_to_all(out, AXES, 0, 0, tiled=True).astype(F32).sum(0)  13 us
    pallas_call x4, Pallas kernels, call(): pl.pallas_call(kernel, out_shape=[pltpu.VMEM(s, t) if stays else jax.Shap...  10.9 us
    all_to_all x1, blocking collectives, gather(): return lax.all_to_all(wide, AXES, 0, 0, tiled=True)  9.88 us
    ppermute x2, starting transfers between devices, along(): lax.ppermute(value, axis, [(source, source + steps) for source in range(f...  6.96 us
    squeeze x1, local copies, waits for them, and re-layouts, shards(): below = along(volumes[0, :, -3:], 'space', 1)  1.03 us
  transfers between devices with their start and end apart: 2, of which 0 were waited for; matrix products, arithmetic and copies ran while one was open for 0% of the time, Pallas kernels for 21%

profile of v4, /device:TPU:0, one launch (start us, length us, event | category | flops | bytes accessed | tf_op | source)
XLA Modules:
  0.0 43.2 jit_solution(6465555872569141123)
XLA Ops:
  0.6 1.0 %slice_bitcast_fusion = bf16[4,3,32,512]{3,2,1,0:T(8,128)(2,1)S(1)} fusion(bf16[1,4,8,32,512]{4,3,2,1,0:T(8,128)(2,1)} %param.7), kind=kLoop, calls=%fused_computation | loop fusion | bytes 786432 | tf_op jit(solution)/shard_map/squeeze | solution.py:330
  1.7 2.4 %collective-permute-start = (bf16[4,3,32,512]{3,2,1,0:T(8,128)(2,1)S(1)}, bf16[4,3,32,512]{3,2,1,0:T(8,128)(2,1)S(1)}, u32[]{:S(2)}, u32[]{:S(2)}) collective-permute-start(bf16[4,3,32,512]{3,2,1,0:T(8,128)(2,1)S(1)} %slice_bitcast_fusion), channel_id=1, source_target_pairs={{0,1},{1,2},{2,3},{3,4},{4,5},{5,6},{6,7},{8,9},{9,10},{10,11},{11... | collective-permute-start | bytes 1179656 | tf_op jit(solution)/shard_map/ppermute | solution.py:27
  4.1 4.4 %shard_map.110 = (bf16[512,512]{1,0:T(8,128)(2,1)S(1)}, bf16[3,128,112]{2,1,0:T(8,128)(2,1)S(1)}, bf16[3,64,288]{2,1,0:T(8,128)(2,1)S(1)}, bf16[384,256]{1,0:T(8...) custom-call(bf16[4,8,32,512]{3,2,1,0:T(8,128)(2,1)} %bitcast.15, ...), custom_call_target="tpu_custom_call" | custom-call | tf_op jit(solution)/shard_map/pallas_call | solution.py:303
  8.5 4.6 %collective-permute-start.1 = (bf16[512,128]{1,0:T(8,128)(2,1)S(1)}, bf16[512,128]{1,0:T(8,128)(2,1)S(1)}, u32[]{:S(2)}, u32[]{:S(2)}) collective-permute-start(bf16[512,128]{1,0:T(8,128)(2,1)S(1)} %get-tuple-element.33), channel_id=1, source_target_pairs={{0,1},{1,2},{2,3},{3,4},{4,5},{5,6},{6,7},{8,9},{9,10},{10,11},{11... | collective-permute-start | bytes 393224 | tf_op jit(solution)/shard_map/ppermute | solution.py:27
  13.1 0.0 collective-permute-done.vh_ref
  13.1 4.5 %shard_map.111 = (bf16[64,2,8,128]{3,2,1,0:T(8,128)(2,1)}, f32[512,128]{1,0:T(8,128)S(1)}, f32[3,128,112]{2,1,0:T(8,128)S(1)}, f32[1024,128]{1,0:T(8,128)S(1)}, ...) custom-call(bf16[4,3,32,512]{3,2,1,0:T(8,128)(2,1)S(1)} %collective-permute-done.vh_ref, ...), custom_call_target="tpu_custom_call" | custom-call | tf_op jit(solution)/shard_map/pallas_call | solution.py:303
  17.6 0.0 collective-permute-done.1.under_ref
  17.6 0.0 copy-start.1
  17.6 0.0 copy-start.2
  17.6 0.0 copy-start
  17.6 1.1 %shard_map.112 = bf16[32,16,128]{2,1,0:T(8,128)(2,1)S(1)} custom-call(bf16[512,128]{1,0:T(8,128)(2,1)S(1)} %collective-permute-done.1.under_ref, bf16[384,256]{1,0:T(8,128)(2,1)S(1)} %get-tuple-element.27.lmat, bf16[3,672,128]{2,1,0:T(8,128)(2,1)S(1)} %get-tuple-element.34.dl_ref, bf16[2,1632,128]{2,1,0:T(8,128)(2,1)S(1)} %get-tuple-element.35.hl_ref, ...), custom_call_target="tpu_custom_call" | custom-call | tf_op jit(solution)/shard_map/pallas_call | solution.py:303
  18.7 13.0 %all_to_all.10 = bf16[32,16,128]{2,1,0:T(8,128)(2,1)S(1)} all-to-all(bf16[32,16,128]{2,1,0:T(8,128)(2,1)S(1)} %shard_map.112), channel_id=1, replica_groups=mesh['dp'=4,'space'=8] {'dp','space'}, dimensions={0} | all-to-all | bytes 262144 | tf_op jit(solution)/shard_map/all_to_all | solution.py:360
  31.7 0.0 copy-done.1
  31.7 0.0 copy-done.2
  31.7 0.6 %divide_convert_fusion = (bf16[1728]{0:T(1024)(128)(2,1)S(1)}, f32[1728]{0:T(1024)}, f32[1728]{0:T(1024)}) fusion(f32[2048]{0:T(1024)S(1)} %bitcast.17, f32[1728]{0:T(1024)S(1)} %copy-done.1, f32[1728]{0:T(1024)S(1)} %copy-done.2), kind=kLoop, calls=%fused_computation.4 | loop fusion | flops 19008 | bytes 38016 | tf_op jit(solution)/shard_map/convert.4
  32.4 9.9 %all_to_all.11.full_ref = bf16[32,16,128]{2,1,0:T(8,128)(2,1)S(1)} all-to-all(bf16[32,16,128]{2,1,0:T(8,128)(2,1)S(1)} %broadcast_in_dim.10), channel_id=1, replica_groups=mesh['dp'=4,'space'=8] {'dp','space'}, dimensions={0} | all-to-all | bytes 262144 | tf_op jit(solution)/shard_map/all_to_all | solution.py:323
  42.2 0.0 copy-done
  42.2 0.9 %shard_map.113 = (f32[864,64]{1,0:T(8,128)}, f32[27,4,32]{2,1,0:T(4,128)}) custom-call(bf16[32,16,128]{2,1,0:T(8,128)(2,1)S(1)} %all_to_all.11.full_ref, f32[864,64]{1,0:T(8,128)S(1)} %bitcast.14), custom_call_target="tpu_custom_call" | custom-call | tf_op jit(solution)/shard_map/pallas_call | solution.py:303
  (5 shorter events, 0.1 us)
Async XLA Ops:
  1.7 11.4 %collective-permute-start = (bf16[4,3,32,512]{3,2,1,0:T(8,128)(2,1)S(1)}, bf16[4,3,32,512]{3,2,1,0:T(8,128)(2,1)S(1)}, u32[]{:S(2)}, u32[]{:S(2)}) collective-permute-start(bf16[4,3,32,512]{3,2,1,0:T(8,128)(2,1)S(1)} %slice_bitcast_fusion), channel_id=1, source_target_pairs={{0,1},{1,2},{2,3},{3,4},{4,5},{5,6},{6,7},{8,9},{9,10},{10,11},{11... | collective-permute-start | bytes 1179656 | tf_op jit(solution)/shard_map/ppermute | solution.py:27
  8.5 9.1 %collective-permute-start.1 = (bf16[512,128]{1,0:T(8,128)(2,1)S(1)}, bf16[512,128]{1,0:T(8,128)(2,1)S(1)}, u32[]{:S(2)}, u32[]{:S(2)}) collective-permute-start(bf16[512,128]{1,0:T(8,128)(2,1)S(1)} %get-tuple-element.33), channel_id=1, source_target_pairs={{0,1},{1,2},{2,3},{3,4},{4,5},{5,6},{6,7},{8,9},{9,10},{10,11},{11... | collective-permute-start | bytes 393224 | tf_op jit(solution)/shard_map/ppermute | solution.py:27
  17.6 14.1 %copy-start.1 = (f32[1728]{0:T(1024)S(1)}, f32[1728]{0:T(1024)}, u32[]{:S(2)}) copy-start(f32[1728]{0:T(1024)} %param.11) | copy-start | bytes 20740
  17.6 14.1 %copy-start.2 = (f32[1728]{0:T(1024)S(1)}, f32[1728]{0:T(1024)}, u32[]{:S(2)}) copy-start(f32[1728]{0:T(1024)} %param.12) | copy-start | bytes 20740
  17.6 24.7 %copy-start = (f32[3,3,3,32,64]{4,3,2,1,0:T(8,128)S(1)}, f32[3,3,3,32,64]{4,3,2,1,0:T(8,128)}, u32[]{:S(2)}) copy-start(f32[3,3,3,32,64]{4,3,2,1,0:T(8,128)} %param.9) | copy-start | bytes 663556

commit v5 on v4

--- a/solution.py
+++ b/solution.py
@@ -57,15 +57,17 @@
 def repack(source, first, count, sel, stage, out, to):
     x = jnp.concatenate([source[:, first + i].reshape(4 * 32, 512) for i in range(count)], axis=0)
     lane = lax.broadcasted_iota(jnp.int32, (32, LANES), 1)
-    for r in range(4):
-        part = nn(x, sel[:, r * LANES:(r + 1) * LANES])
-        for i in range(count):
-            for c in range(4):
-                block = part[i * 128 + c * 32:i * 128 + c * 32 + 32]
-                stage[i, pl.ds(SLOTS + (r + 1) * 4 + c, 32, stride=SLOTS), :] = block
-                if r == 3:
-                    moved = jnp.where(lane == 0, 0.0, pltpu.roll(block, 1, 1))
-                    stage[i, pl.ds(SLOTS + c, 32, stride=SLOTS), :] = moved
+    for r0 in range(0, 4, 2):
+        parts = nn(x, sel[:, r0 * LANES:(r0 + 2) * LANES])
+        for r in range(r0, r0 + 2):
+            part = parts[:, (r - r0) * LANES:(r - r0 + 1) * LANES]
+            for i in range(count):
+                for c in range(4):
+                    block = part[i * 128 + c * 32:i * 128 + c * 32 + 32]
+                    stage[i, pl.ds(SLOTS + (r + 1) * 4 + c, 32, stride=SLOTS), :] = block
+                    if r == 3:
+                        moved = jnp.where(lane == 0, 0.0, pltpu.roll(block, 1, 1))
+                        stage[i, pl.ds(SLOTS + c, 32, stride=SLOTS), :] = moved
     for i in range(count):
         out[to + i] = stage[i].astype(BF)
 
@@ -263,15 +265,16 @@
         for m in range(8):
             acc += nt(d1[m * 128:m * 128 + 128], rows_of(m))
         wide = jnp.concatenate([acc, jnp.zeros((128, LANES - REACH), F32)], axis=1)
+        part = jnp.zeros((32, LANES), F32)
+        for i in range(2):
+            for p in range(2):
+                block = wide[(2 * i + p) * 32:(2 * i + p) * 32 + 32]
+                shift = -(2 * i * SLOTS + 8 * p) % LANES
+                part += block if shift == 0 else pltpu.roll(block, shift, 1)
         for dy in range(3):
             to = (dz * 3 + dy) * 12
-            part = jnp.zeros((32, LANES), F32)
-            for i in range(2):
-                for p in range(2):
-                    block = wide[(2 * i + p) * 32:(2 * i + p) * 32 + 32]
-                    shift = (to - ((2 * i + dy) * SLOTS + 8 * p)) % LANES
-                    part += block if shift == 0 else pltpu.roll(block, shift, 1)
-            total = jnp.where((lane >= to) & (lane < to + 12), part, total)
+            shift = (to - dy * SLOTS) % LANES
+            total = jnp.where((lane >= to) & (lane < to + 12), part if shift == 0 else pltpu.roll(part, shift, 1), total)
     if not packed:
         out_ref[...] = total
         return

time: 43.4 us -> 43.3 us (level)
  Pallas kernels: 10.9 us -> 10.3 us
    pallas_call x4, Pallas kernels: 10.9 us -> 10.3 us  [call(): pl.pallas_call(kernel, out_shape=[pltpu.VMEM(s, t) if stays else jax.Shap...]
    all_to_all x1, blocking collectives: 13 us -> 13.5 us  [shards(): both = lax.all_to_all(out, AXES, 0, 0, tiled=True).astype(F32).sum(0)]
  transfers between devices with their start and end apart: 2 -> 2, of which waited for: 0 -> 0; matrix products, arithmetic and copies ran while one was open for 0% -> 0% of each run, Pallas kernels for 21% -> 19%
where the time goes in v5:
time: 43.3 us; the launch traced here: 43 us
  blocking collectives  23.3 us (54%)
  Pallas kernels  10.3 us (24%)
  starting transfers between devices  6.96 us (16%)
  local copies, waits for them, and re-layouts  1.07 us (2%)
  between operations  0.72 us (2%)
  other arithmetic  0.67 us (2%)
    all_to_all x1, blocking collectives, shards(): both = lax.all_to_all(out, AXES, 0, 0, tiled=True).astype(F32).sum(0)  13.5 us
    pallas_call x4, Pallas kernels, call(): pl.pallas_call(kernel, out_shape=[pltpu.VMEM(s, t) if stays else jax.Shap...  10.3 us
    all_to_all x1, blocking collectives, gather(): return lax.all_to_all(wide, AXES, 0, 0, tiled=True)  9.88 us
    ppermute x2, starting transfers between devices, along(): lax.ppermute(value, axis, [(source, source + steps) for source in range(f...  6.96 us
    squeeze x1, local copies, waits for them, and re-layouts, shards(): below = along(volumes[0, :, -3:], 'space', 1)  1.03 us
  transfers between devices with their start and end apart: 2, of which 0 were waited for; matrix products, arithmetic and copies ran while one was open for 0% of the time, Pallas kernels for 19%

profile of v5, /device:TPU:0, one launch (start us, length us, event | category | flops | bytes accessed | tf_op | source)
XLA Modules:
  0.0 43.0 jit_solution(1831856354590588491)
XLA Ops:
  0.6 1.0 %slice_bitcast_fusion = bf16[4,3,32,512]{3,2,1,0:T(8,128)(2,1)S(1)} fusion(bf16[1,4,8,32,512]{4,3,2,1,0:T(8,128)(2,1)} %param.7), kind=kLoop, calls=%fused_computation | loop fusion | bytes 786432 | tf_op jit(solution)/shard_map/squeeze | solution.py:333
  1.7 2.4 %collective-permute-start = (bf16[4,3,32,512]{3,2,1,0:T(8,128)(2,1)S(1)}, bf16[4,3,32,512]{3,2,1,0:T(8,128)(2,1)S(1)}, u32[]{:S(2)}, u32[]{:S(2)}) collective-permute-start(bf16[4,3,32,512]{3,2,1,0:T(8,128)(2,1)S(1)} %slice_bitcast_fusion), channel_id=1, source_target_pairs={{0,1},{1,2},{2,3},{3,4},{4,5},{5,6},{6,7},{8,9},{9,10},{10,11},{11... | collective-permute-start | bytes 1179656 | tf_op jit(solution)/shard_map/ppermute | solution.py:27
  4.1 3.9 %shard_map.110 = (bf16[512,512]{1,0:T(8,128)(2,1)S(1)}, bf16[3,128,112]{2,1,0:T(8,128)(2,1)S(1)}, bf16[3,64,288]{2,1,0:T(8,128)(2,1)S(1)}, bf16[384,256]{1,0:T(8...) custom-call(bf16[4,8,32,512]{3,2,1,0:T(8,128)(2,1)} %bitcast.15, ...), custom_call_target="tpu_custom_call" | custom-call | tf_op jit(solution)/shard_map/pallas_call | solution.py:306
  8.0 4.6 %collective-permute-start.1 = (bf16[512,128]{1,0:T(8,128)(2,1)S(1)}, bf16[512,128]{1,0:T(8,128)(2,1)S(1)}, u32[]{:S(2)}, u32[]{:S(2)}) collective-permute-start(bf16[512,128]{1,0:T(8,128)(2,1)S(1)} %get-tuple-element.33), channel_id=1, source_target_pairs={{0,1},{1,2},{2,3},{3,4},{4,5},{5,6},{6,7},{8,9},{9,10},{10,11},{11... | collective-permute-start | bytes 393224 | tf_op jit(solution)/shard_map/ppermute | solution.py:27
  12.6 0.0 collective-permute-done.vh_ref
  12.6 4.3 %shard_map.111 = (bf16[64,2,8,128]{3,2,1,0:T(8,128)(2,1)}, f32[512,128]{1,0:T(8,128)S(1)}, f32[3,128,112]{2,1,0:T(8,128)S(1)}, f32[1024,128]{1,0:T(8,128)S(1)}, ...) custom-call(bf16[4,3,32,512]{3,2,1,0:T(8,128)(2,1)S(1)} %collective-permute-done.vh_ref, ...), custom_call_target="tpu_custom_call" | custom-call | tf_op jit(solution)/shard_map/pallas_call | solution.py:306
  16.9 0.0 collective-permute-done.1.under_ref
  16.9 0.0 copy-start.1
  16.9 0.0 copy-start.2
  16.9 0.0 copy-start
  16.9 1.1 %shard_map.112 = bf16[32,16,128]{2,1,0:T(8,128)(2,1)S(1)} custom-call(bf16[512,128]{1,0:T(8,128)(2,1)S(1)} %collective-permute-done.1.under_ref, bf16[384,256]{1,0:T(8,128)(2,1)S(1)} %get-tuple-element.27.lmat, bf16[3,672,128]{2,1,0:T(8,128)(2,1)S(1)} %get-tuple-element.34.dl_ref, bf16[2,1632,128]{2,1,0:T(8,128)(2,1)S(1)} %get-tuple-element.35.hl_ref, ...), custom_call_target="tpu_custom_call" | custom-call | tf_op jit(solution)/shard_map/pallas_call | solution.py:306
  18.0 13.5 %all_to_all.10 = bf16[32,16,128]{2,1,0:T(8,128)(2,1)S(1)} all-to-all(bf16[32,16,128]{2,1,0:T(8,128)(2,1)S(1)} %shard_map.112), channel_id=1, replica_groups=mesh['dp'=4,'space'=8] {'dp','space'}, dimensions={0} | all-to-all | bytes 262144 | tf_op jit(solution)/shard_map/all_to_all | solution.py:363
  31.5 0.0 copy-done.1
  31.6 0.0 copy-done.2
  31.6 0.6 %divide_convert_fusion = (bf16[1728]{0:T(1024)(128)(2,1)S(1)}, f32[1728]{0:T(1024)}, f32[1728]{0:T(1024)}) fusion(f32[2048]{0:T(1024)S(1)} %bitcast.17, f32[1728]{0:T(1024)S(1)} %copy-done.1, f32[1728]{0:T(1024)S(1)} %copy-done.2), kind=kLoop, calls=%fused_computation.4 | loop fusion | flops 19008 | bytes 38016 | tf_op jit(solution)/shard_map/convert.4
  32.2 9.9 %all_to_all.11.full_ref = bf16[32,16,128]{2,1,0:T(8,128)(2,1)S(1)} all-to-all(bf16[32,16,128]{2,1,0:T(8,128)(2,1)S(1)} %broadcast_in_dim.10), channel_id=1, replica_groups=mesh['dp'=4,'space'=8] {'dp','space'}, dimensions={0} | all-to-all | bytes 262144 | tf_op jit(solution)/shard_map/all_to_all | solution.py:326
  42.1 0.0 copy-done
  42.1 0.9 %shard_map.113 = (f32[864,64]{1,0:T(8,128)}, f32[27,4,32]{2,1,0:T(4,128)}) custom-call(bf16[32,16,128]{2,1,0:T(8,128)(2,1)S(1)} %all_to_all.11.full_ref, f32[864,64]{1,0:T(8,128)S(1)} %bitcast.14), custom_call_target="tpu_custom_call" | custom-call | tf_op jit(solution)/shard_map/pallas_call | solution.py:306
  (5 shorter events, 0.1 us)
Async XLA Ops:
  1.7 10.9 %collective-permute-start = (bf16[4,3,32,512]{3,2,1,0:T(8,128)(2,1)S(1)}, bf16[4,3,32,512]{3,2,1,0:T(8,128)(2,1)S(1)}, u32[]{:S(2)}, u32[]{:S(2)}) collective-permute-start(bf16[4,3,32,512]{3,2,1,0:T(8,128)(2,1)S(1)} %slice_bitcast_fusion), channel_id=1, source_target_pairs={{0,1},{1,2},{2,3},{3,4},{4,5},{5,6},{6,7},{8,9},{9,10},{10,11},{11... | collective-permute-start | bytes 1179656 | tf_op jit(solution)/shard_map/ppermute | solution.py:27
  8.0 8.9 %collective-permute-start.1 = (bf16[512,128]{1,0:T(8,128)(2,1)S(1)}, bf16[512,128]{1,0:T(8,128)(2,1)S(1)}, u32[]{:S(2)}, u32[]{:S(2)}) collective-permute-start(bf16[512,128]{1,0:T(8,128)(2,1)S(1)} %get-tuple-element.33), channel_id=1, source_target_pairs={{0,1},{1,2},{2,3},{3,4},{4,5},{5,6},{6,7},{8,9},{9,10},{10,11},{11... | collective-permute-start | bytes 393224 | tf_op jit(solution)/shard_map/ppermute | solution.py:27
  16.9 14.6 %copy-start.1 = (f32[1728]{0:T(1024)S(1)}, f32[1728]{0:T(1024)}, u32[]{:S(2)}) copy-start(f32[1728]{0:T(1024)} %param.11) | copy-start | bytes 20740
  16.9 14.7 %copy-start.2 = (f32[1728]{0:T(1024)S(1)}, f32[1728]{0:T(1024)}, u32[]{:S(2)}) copy-start(f32[1728]{0:T(1024)} %param.12) | copy-start | bytes 20740
  16.9 25.2 %copy-start = (f32[3,3,3,32,64]{4,3,2,1,0:T(8,128)S(1)}, f32[3,3,3,32,64]{4,3,2,1,0:T(8,128)}, u32[]{:S(2)}) copy-start(f32[3,3,3,32,64]{4,3,2,1,0:T(8,128)} %param.9) | copy-start | bytes 663556

commit v6 on v5

--- a/solution.py
+++ b/solution.py
@@ -254,16 +254,17 @@
         d2h[y * 128:y * 128 + 64] = low
         d2h[y * 128 + 64:y * 128 + 128] = left.astype(BF)
     for m in range(8):
+        if m % 2 == 0:
+            more = nn(lmat[256:384], beside(d2h[m * 128:m * 128 + 256], d2h[m * 128 + 128:m * 128 + 384]))
         rows = slice(m * 128, m * 128 + 128)
-        grad = grad_ref[rows] + nn(lmat[256:384], d2h[m * 128:m * 128 + 256])
+        grad = grad_ref[rows] + more[:, (m % 2) * LANES:(m % 2 + 1) * LANES]
         d1[rows] = (grad * slopes(hl_ref, 0, m)).astype(BF)
     lane = lax.broadcasted_iota(jnp.int32, (32, LANES), 1)
     total = jnp.zeros((32, LANES), F32)
     for dz in range(3):
         acc = g1_ref[dz]
         rows_of = pair_rows((dl_ref, dz))
-        for m in range(8):
-            acc += nt(d1[m * 128:m * 128 + 128], rows_of(m))
+        acc += nt(beside(*[d1[m * 128:m * 128 + 128] for m in range(8)]), beside(*[rows_of(m) for m in range(8)]))
         wide = jnp.concatenate([acc, jnp.zeros((128, LANES - REACH), F32)], axis=1)
         part = jnp.zeros((32, LANES), F32)
         for i in range(2):

time: 43.3 us -> 42.9 us (level)
  no operation moved by 1% of the time
where the time goes in v6:
time: 42.9 us; the launch traced here: 42.7 us
  blocking collectives  23.3 us (54%)
  Pallas kernels  9.92 us (23%)
  starting transfers between devices  6.96 us (16%)
  local copies, waits for them, and re-layouts  1.07 us (2%)
  between operations  0.72 us (2%)
  other arithmetic  0.67 us (2%)
    all_to_all x1, blocking collectives, shards(): both = lax.all_to_all(out, AXES, 0, 0, tiled=True).astype(F32).sum(0)  13.5 us
    pallas_call x4, Pallas kernels, call(): pl.pallas_call(kernel, out_shape=[pltpu.VMEM(s, t) if stays else jax.Shap...  9.92 us
    all_to_all x1, blocking collectives, gather(): return lax.all_to_all(wide, AXES, 0, 0, tiled=True)  9.88 us
    ppermute x2, starting transfers between devices, along(): lax.ppermute(value, axis, [(source, source + steps) for source in range(f...  6.96 us
    squeeze x1, local copies, waits for them, and re-layouts, shards(): below = along(volumes[0, :, -3:], 'space', 1)  1.03 us
  transfers between devices with their start and end apart: 2, of which 0 were waited for; matrix products, arithmetic and copies ran while one was open for 0% of the time, Pallas kernels for 19%

profile of v6, /device:TPU:0, one launch (start us, length us, event | category | flops | bytes accessed | tf_op | source)
XLA Modules:
  0.0 42.7 jit_solution(9307573446103367805)
XLA Ops:
  0.6 1.0 %slice_bitcast_fusion = bf16[4,3,32,512]{3,2,1,0:T(8,128)(2,1)S(1)} fusion(bf16[1,4,8,32,512]{4,3,2,1,0:T(8,128)(2,1)} %param.7), kind=kLoop, calls=%fused_computation | loop fusion | bytes 786432 | tf_op jit(solution)/shard_map/squeeze | solution.py:334
  1.7 2.4 %collective-permute-start = (bf16[4,3,32,512]{3,2,1,0:T(8,128)(2,1)S(1)}, bf16[4,3,32,512]{3,2,1,0:T(8,128)(2,1)S(1)}, u32[]{:S(2)}, u32[]{:S(2)}) collective-permute-start(bf16[4,3,32,512]{3,2,1,0:T(8,128)(2,1)S(1)} %slice_bitcast_fusion), channel_id=1, source_target_pairs={{0,1},{1,2},{2,3},{3,4},{4,5},{5,6},{6,7},{8,9},{9,10},{10,11},{11... | collective-permute-start | bytes 1179656 | tf_op jit(solution)/shard_map/ppermute | solution.py:27
  4.1 3.9 %shard_map.110 = (bf16[512,512]{1,0:T(8,128)(2,1)S(1)}, bf16[3,128,112]{2,1,0:T(8,128)(2,1)S(1)}, bf16[3,64,288]{2,1,0:T(8,128)(2,1)S(1)}, bf16[384,256]{1,0:T(8...) custom-call(bf16[4,8,32,512]{3,2,1,0:T(8,128)(2,1)} %bitcast.15, ...), custom_call_target="tpu_custom_call" | custom-call | tf_op jit(solution)/shard_map/pallas_call | solution.py:307
  8.0 4.6 %collective-permute-start.1 = (bf16[512,128]{1,0:T(8,128)(2,1)S(1)}, bf16[512,128]{1,0:T(8,128)(2,1)S(1)}, u32[]{:S(2)}, u32[]{:S(2)}) collective-permute-start(bf16[512,128]{1,0:T(8,128)(2,1)S(1)} %get-tuple-element.33), channel_id=1, source_target_pairs={{0,1},{1,2},{2,3},{3,4},{4,5},{5,6},{6,7},{8,9},{9,10},{10,11},{11... | collective-permute-start | bytes 393224 | tf_op jit(solution)/shard_map/ppermute | solution.py:27
  12.6 0.0 collective-permute-done.vh_ref
  12.6 4.3 %shard_map.111 = (bf16[64,2,8,128]{3,2,1,0:T(8,128)(2,1)}, f32[512,128]{1,0:T(8,128)S(1)}, f32[3,128,112]{2,1,0:T(8,128)S(1)}, f32[1024,128]{1,0:T(8,128)S(1)}, ...) custom-call(bf16[4,3,32,512]{3,2,1,0:T(8,128)(2,1)S(1)} %collective-permute-done.vh_ref, ...), custom_call_target="tpu_custom_call" | custom-call | tf_op jit(solution)/shard_map/pallas_call | solution.py:307
  16.9 0.0 collective-permute-done.1.under_ref
  16.9 0.0 copy-start.1
  16.9 0.0 copy-start.2
  16.9 0.0 copy-start
  16.9 0.8 %shard_map.112 = bf16[32,16,128]{2,1,0:T(8,128)(2,1)S(1)} custom-call(bf16[512,128]{1,0:T(8,128)(2,1)S(1)} %collective-permute-done.1.under_ref, bf16[384,256]{1,0:T(8,128)(2,1)S(1)} %get-tuple-element.27.lmat, bf16[3,672,128]{2,1,0:T(8,128)(2,1)S(1)} %get-tuple-element.34.dl_ref, bf16[2,1632,128]{2,1,0:T(8,128)(2,1)S(1)} %get-tuple-element.35.hl_ref, ...), custom_call_target="tpu_custom_call" | custom-call | tf_op jit(solution)/shard_map/pallas_call | solution.py:307
  17.7 13.5 %all_to_all.10 = bf16[32,16,128]{2,1,0:T(8,128)(2,1)S(1)} all-to-all(bf16[32,16,128]{2,1,0:T(8,128)(2,1)S(1)} %shard_map.112), channel_id=1, replica_groups=mesh['dp'=4,'space'=8] {'dp','space'}, dimensions={0} | all-to-all | bytes 262144 | tf_op jit(solution)/shard_map/all_to_all | solution.py:364
  31.2 0.0 copy-done.1
  31.2 0.0 copy-done.2
  31.2 0.6 %divide_convert_fusion = (bf16[1728]{0:T(1024)(128)(2,1)S(1)}, f32[1728]{0:T(1024)}, f32[1728]{0:T(1024)}) fusion(f32[2048]{0:T(1024)S(1)} %bitcast.17, f32[1728]{0:T(1024)S(1)} %copy-done.1, f32[1728]{0:T(1024)S(1)} %copy-done.2), kind=kLoop, calls=%fused_computation.4 | loop fusion | flops 19008 | bytes 38016 | tf_op jit(solution)/shard_map/convert.4
  31.9 9.9 %all_to_all.11.full_ref = bf16[32,16,128]{2,1,0:T(8,128)(2,1)S(1)} all-to-all(bf16[32,16,128]{2,1,0:T(8,128)(2,1)S(1)} %broadcast_in_dim.10), channel_id=1, replica_groups=mesh['dp'=4,'space'=8] {'dp','space'}, dimensions={0} | all-to-all | bytes 262144 | tf_op jit(solution)/shard_map/all_to_all | solution.py:327
  41.8 0.0 copy-done
  41.8 0.9 %shard_map.113 = (f32[864,64]{1,0:T(8,128)}, f32[27,4,32]{2,1,0:T(4,128)}) custom-call(bf16[32,16,128]{2,1,0:T(8,128)(2,1)S(1)} %all_to_all.11.full_ref, f32[864,64]{1,0:T(8,128)S(1)} %bitcast.14), custom_call_target="tpu_custom_call" | custom-call | tf_op jit(solution)/shard_map/pallas_call | solution.py:307
  (5 shorter events, 0.1 us)
Async XLA Ops:
  1.7 10.9 %collective-permute-start = (bf16[4,3,32,512]{3,2,1,0:T(8,128)(2,1)S(1)}, bf16[4,3,32,512]{3,2,1,0:T(8,128)(2,1)S(1)}, u32[]{:S(2)}, u32[]{:S(2)}) collective-permute-start(bf16[4,3,32,512]{3,2,1,0:T(8,128)(2,1)S(1)} %slice_bitcast_fusion), channel_id=1, source_target_pairs={{0,1},{1,2},{2,3},{3,4},{4,5},{5,6},{6,7},{8,9},{9,10},{10,11},{11... | collective-permute-start | bytes 1179656 | tf_op jit(solution)/shard_map/ppermute | solution.py:27
  8.0 8.9 %collective-permute-start.1 = (bf16[512,128]{1,0:T(8,128)(2,1)S(1)}, bf16[512,128]{1,0:T(8,128)(2,1)S(1)}, u32[]{:S(2)}, u32[]{:S(2)}) collective-permute-start(bf16[512,128]{1,0:T(8,128)(2,1)S(1)} %get-tuple-element.33), channel_id=1, source_target_pairs={{0,1},{1,2},{2,3},{3,4},{4,5},{5,6},{6,7},{8,9},{9,10},{10,11},{11... | collective-permute-start | bytes 393224 | tf_op jit(solution)/shard_map/ppermute | solution.py:27
  16.9 14.3 %copy-start.1 = (f32[1728]{0:T(1024)S(1)}, f32[1728]{0:T(1024)}, u32[]{:S(2)}) copy-start(f32[1728]{0:T(1024)} %param.11) | copy-start | bytes 20740
  16.9 14.3 %copy-start.2 = (f32[1728]{0:T(1024)S(1)}, f32[1728]{0:T(1024)}, u32[]{:S(2)}) copy-start(f32[1728]{0:T(1024)} %param.12) | copy-start | bytes 20740
  16.9 24.9 %copy-start = (f32[3,3,3,32,64]{4,3,2,1,0:T(8,128)S(1)}, f32[3,3,3,32,64]{4,3,2,1,0:T(8,128)}, u32[]{:S(2)}) copy-start(f32[3,3,3,32,64]{4,3,2,1,0:T(8,128)} %param.9) | copy-start | bytes 663556

commit v7 on v6

--- a/solution.py
+++ b/solution.py
@@ -108,9 +108,9 @@
     lane = lax.broadcasted_iota(jnp.int32, (64, LANES), 1)
     rows_c[...] = cot_ref[:, z].astype(F32).reshape(512, LANES)
     for y in range(8):
-        acc = nn(w2t[0], planes[0][0][planes[0][1], y * 192:y * 192 + 288])
-        acc += nn(w2t[1], planes[1][0][planes[1][1], y * 192:y * 192 + 288])
-        acc += nn(w2t[2], planes[2][0][planes[2][1], y * 192:y * 192 + 288])
+        if y % 2 == 0:
+            both = sum(nn(w2t[dz], beside(*[ref[at, k * 192:k * 192 + 288] for k in (y, y + 1)])) for dz, (ref, at) in enumerate(planes))
+        acc = both[:, (y % 2) * LANES:(y % 2 + 1) * LANES]
         rows_a[pl.ds(y, 64, stride=8), :] = leaky(acc)
         delta = rows_c[pl.ds(y, 64, stride=8), :] * jnp.where(acc > 0, 1.0, SLOPE)
         left = jnp.where(lane == LANES - 1, 0.0, pltpu.roll(delta, LANES - 1, 1))

time: 42.9 us -> 42.9 us (level)
  no operation moved by 1% of the time
where the time goes in v7:
time: 42.9 us; the launch traced here: 42.7 us
  blocking collectives  23.3 us (54%)
  Pallas kernels  9.95 us (23%)
  starting transfers between devices  6.96 us (16%)
  local copies, waits for them, and re-layouts  1.07 us (2%)
  between operations  0.72 us (2%)
  other arithmetic  0.67 us (2%)
    all_to_all x1, blocking collectives, shards(): both = lax.all_to_all(out, AXES, 0, 0, tiled=True).astype(F32).sum(0)  13.4 us
    pallas_call x4, Pallas kernels, call(): pl.pallas_call(kernel, out_shape=[pltpu.VMEM(s, t) if stays else jax.Shap...  9.95 us
    all_to_all x1, blocking collectives, gather(): return lax.all_to_all(wide, AXES, 0, 0, tiled=True)  9.88 us
    ppermute x2, starting transfers between devices, along(): lax.ppermute(value, axis, [(source, source + steps) for source in range(f...  6.96 us
    squeeze x1, local copies, waits for them, and re-layouts, shards(): below = along(volumes[0, :, -3:], 'space', 1)  1.03 us
  transfers between devices with their start and end apart: 2, of which 0 were waited for; matrix products, arithmetic and copies ran while one was open for 0% of the time, Pallas kernels for 19%

profile of v7, /device:TPU:0, one launch (start us, length us, event | category | flops | bytes accessed | tf_op | source)
XLA Modules:
  0.0 42.7 jit_solution(4744691747903213992)
XLA Ops:
  0.6 1.0 %slice_bitcast_fusion = bf16[4,3,32,512]{3,2,1,0:T(8,128)(2,1)S(1)} fusion(bf16[1,4,8,32,512]{4,3,2,1,0:T(8,128)(2,1)} %param.7), kind=kLoop, calls=%fused_computation | loop fusion | bytes 786432 | tf_op jit(solution)/shard_map/squeeze | solution.py:334
  1.7 2.4 %collective-permute-start = (bf16[4,3,32,512]{3,2,1,0:T(8,128)(2,1)S(1)}, bf16[4,3,32,512]{3,2,1,0:T(8,128)(2,1)S(1)}, u32[]{:S(2)}, u32[]{:S(2)}) collective-permute-start(bf16[4,3,32,512]{3,2,1,0:T(8,128)(2,1)S(1)} %slice_bitcast_fusion), channel_id=1, source_target_pairs={{0,1},{1,2},{2,3},{3,4},{4,5},{5,6},{6,7},{8,9},{9,10},{10,11},{11... | collective-permute-start | bytes 1179656 | tf_op jit(solution)/shard_map/ppermute | solution.py:27
  4.1 3.9 %shard_map.110 = (bf16[512,512]{1,0:T(8,128)(2,1)S(1)}, bf16[3,128,112]{2,1,0:T(8,128)(2,1)S(1)}, bf16[3,64,288]{2,1,0:T(8,128)(2,1)S(1)}, bf16[384,256]{1,0:T(8...) custom-call(bf16[4,8,32,512]{3,2,1,0:T(8,128)(2,1)} %bitcast.15, ...), custom_call_target="tpu_custom_call" | custom-call | tf_op jit(solution)/shard_map/pallas_call | solution.py:307
  8.0 4.6 %collective-permute-start.1 = (bf16[512,128]{1,0:T(8,128)(2,1)S(1)}, bf16[512,128]{1,0:T(8,128)(2,1)S(1)}, u32[]{:S(2)}, u32[]{:S(2)}) collective-permute-start(bf16[512,128]{1,0:T(8,128)(2,1)S(1)} %get-tuple-element.33), channel_id=1, source_target_pairs={{0,1},{1,2},{2,3},{3,4},{4,5},{5,6},{6,7},{8,9},{9,10},{10,11},{11... | collective-permute-start | bytes 393224 | tf_op jit(solution)/shard_map/ppermute | solution.py:27
  12.6 0.0 collective-permute-done.vh_ref
  12.6 4.3 %shard_map.111 = (bf16[64,2,8,128]{3,2,1,0:T(8,128)(2,1)}, f32[512,128]{1,0:T(8,128)S(1)}, f32[3,128,112]{2,1,0:T(8,128)S(1)}, f32[1024,128]{1,0:T(8,128)S(1)}, ...) custom-call(bf16[4,3,32,512]{3,2,1,0:T(8,128)(2,1)S(1)} %collective-permute-done.vh_ref, ...), custom_call_target="tpu_custom_call" | custom-call | tf_op jit(solution)/shard_map/pallas_call | solution.py:307
  16.9 0.0 collective-permute-done.1.under_ref
  16.9 0.0 copy-start.1
  16.9 0.0 copy-start.2
  16.9 0.0 copy-start
  16.9 0.8 %shard_map.112 = bf16[32,16,128]{2,1,0:T(8,128)(2,1)S(1)} custom-call(bf16[512,128]{1,0:T(8,128)(2,1)S(1)} %collective-permute-done.1.under_ref, bf16[384,256]{1,0:T(8,128)(2,1)S(1)} %get-tuple-element.27.lmat, bf16[3,672,128]{2,1,0:T(8,128)(2,1)S(1)} %get-tuple-element.34.dl_ref, bf16[2,1632,128]{2,1,0:T(8,128)(2,1)S(1)} %get-tuple-element.35.hl_ref, ...), custom_call_target="tpu_custom_call" | custom-call | tf_op jit(solution)/shard_map/pallas_call | solution.py:307
  17.7 13.4 %all_to_all.10 = bf16[32,16,128]{2,1,0:T(8,128)(2,1)S(1)} all-to-all(bf16[32,16,128]{2,1,0:T(8,128)(2,1)S(1)} %shard_map.112), channel_id=1, replica_groups=mesh['dp'=4,'space'=8] {'dp','space'}, dimensions={0} | all-to-all | bytes 262144 | tf_op jit(solution)/shard_map/all_to_all | solution.py:364
  31.2 0.0 copy-done.1
  31.2 0.0 copy-done.2
  31.2 0.6 %divide_convert_fusion = (bf16[1728]{0:T(1024)(128)(2,1)S(1)}, f32[1728]{0:T(1024)}, f32[1728]{0:T(1024)}) fusion(f32[2048]{0:T(1024)S(1)} %bitcast.17, f32[1728]{0:T(1024)S(1)} %copy-done.1, f32[1728]{0:T(1024)S(1)} %copy-done.2), kind=kLoop, calls=%fused_computation.4 | loop fusion | flops 19008 | bytes 38016 | tf_op jit(solution)/shard_map/convert.4
  31.9 9.9 %all_to_all.11.full_ref = bf16[32,16,128]{2,1,0:T(8,128)(2,1)S(1)} all-to-all(bf16[32,16,128]{2,1,0:T(8,128)(2,1)S(1)} %broadcast_in_dim.10), channel_id=1, replica_groups=mesh['dp'=4,'space'=8] {'dp','space'}, dimensions={0} | all-to-all | bytes 262144 | tf_op jit(solution)/shard_map/all_to_all | solution.py:327
  41.8 0.0 copy-done
  41.8 0.9 %shard_map.113 = (f32[864,64]{1,0:T(8,128)}, f32[27,4,32]{2,1,0:T(4,128)}) custom-call(bf16[32,16,128]{2,1,0:T(8,128)(2,1)S(1)} %all_to_all.11.full_ref, f32[864,64]{1,0:T(8,128)S(1)} %bitcast.14), custom_call_target="tpu_custom_call" | custom-call | tf_op jit(solution)/shard_map/pallas_call | solution.py:307
  (5 shorter events, 0.1 us)
Async XLA Ops:
  1.7 10.9 %collective-permute-start = (bf16[4,3,32,512]{3,2,1,0:T(8,128)(2,1)S(1)}, bf16[4,3,32,512]{3,2,1,0:T(8,128)(2,1)S(1)}, u32[]{:S(2)}, u32[]{:S(2)}) collective-permute-start(bf16[4,3,32,512]{3,2,1,0:T(8,128)(2,1)S(1)} %slice_bitcast_fusion), channel_id=1, source_target_pairs={{0,1},{1,2},{2,3},{3,4},{4,5},{5,6},{6,7},{8,9},{9,10},{10,11},{11... | collective-permute-start | bytes 1179656 | tf_op jit(solution)/shard_map/ppermute | solution.py:27
  8.0 8.9 %collective-permute-start.1 = (bf16[512,128]{1,0:T(8,128)(2,1)S(1)}, bf16[512,128]{1,0:T(8,128)(2,1)S(1)}, u32[]{:S(2)}, u32[]{:S(2)}) collective-permute-start(bf16[512,128]{1,0:T(8,128)(2,1)S(1)} %get-tuple-element.33), channel_id=1, source_target_pairs={{0,1},{1,2},{2,3},{3,4},{4,5},{5,6},{6,7},{8,9},{9,10},{10,11},{11... | collective-permute-start | bytes 393224 | tf_op jit(solution)/shard_map/ppermute | solution.py:27
  16.9 14.3 %copy-start.1 = (f32[1728]{0:T(1024)S(1)}, f32[1728]{0:T(1024)}, u32[]{:S(2)}) copy-start(f32[1728]{0:T(1024)} %param.11) | copy-start | bytes 20740
  16.9 14.3 %copy-start.2 = (f32[1728]{0:T(1024)S(1)}, f32[1728]{0:T(1024)}, u32[]{:S(2)}) copy-start(f32[1728]{0:T(1024)} %param.12) | copy-start | bytes 20740
  16.9 24.8 %copy-start = (f32[3,3,3,32,64]{4,3,2,1,0:T(8,128)S(1)}, f32[3,3,3,32,64]{4,3,2,1,0:T(8,128)}, u32[]{:S(2)}) copy-start(f32[3,3,3,32,64]{4,3,2,1,0:T(8,128)} %param.9) | copy-start | bytes 663556
